TPU v7x, 32 devices: a whole 2x2x4 slice. The times are simulated.
32 devices in a mesh: groups: 2 (over y), rec: 4 (over z), lig: 2 (over x), fft: 2 (over core).
Axes of the slice: x: 2, y: 2, z: 4, core: 2. Of those that a mesh axis runs over, the one named last changes fastest.
Arguments:
- receptor_occupancy: int32 [16, 4, 64, 4096], P(('groups', 'rec', 'lig'), None, 'fft'), parts along dimension 0, may hold values from 0 to 3
- ligand_occupancy: int32 [16, 4, 64, 4096], P(('groups', 'rec', 'lig'), None, 'fft'), parts along dimension 0, may hold values from 0 to 3
- rot_index: int32 [16], P(('groups', 'rec', 'lig')), parts along dimension 0, may hold values from 0 to 3
- receptor_extent: int32 [16], P(('groups', 'rec', 'lig')), parts along dimension 0, may hold values from 16 to 64, as said below
- channel_weight: float32 [4], replicated, may hold values from -1 to 2
Outputs:
- plane_top: float32 [16, 3, 2, 64], P(('groups', 'rec', 'lig'), None, None, 'fft'), parts along dimension 0
There are 2 independent parts, one for each index of `groups`. A program takes and returns all parts, laid end to end along the dimension named above; an argument that names none is the same for every part. Nothing has to cross between parts.
Inputs may be any that keep to these rules, and one draw needn't show every extreme that they name: `rot_index`: quarter turns. `receptor_extent`: some receptor has extent 64.
All inputs are finite; a program needn't handle non-finite values.
Results may differ from a plain program's by a relative error of at most 0.0062.
Values may be sent and summed in bfloat16 or wider, within the bound.
A program may use at most 128 MiB of HBM per device.

v0:
```python
import math

import jax
import jax.numpy as jnp
import numpy as np
from jax import lax
from jax.experimental import pallas as pl
from jax.experimental.pallas import tpu as pltpu
from jax.sharding import PartitionSpec as P


REC_STEPS = 3
LIG_STEPS = 2
F32 = jnp.float32
BF16 = jnp.bfloat16
VMEM_BYTES = 20 * 1024 * 1024


def passed_along(value, axis, steps):
    count = lax.axis_size(axis)
    pairs = [(source, (source + steps) % count) for source in range(count)]
    return lax.ppermute(value, axis, pairs)


def trig_tables(cells):
    indices = np.arange(cells)
    phases = indices[:, None] * indices[None, :] % cells
    angles = phases.astype(np.float32) * np.float32(2.0 * math.pi / cells)
    return np.cos(angles), np.sin(angles)


def lane_mixes(real, imag):
    first = np.block([[real, imag], [-imag, real]])
    second = np.block([[-imag, real], [-real, -imag]])
    return np.concatenate([first, second], axis=0)


def make_tables(cells, half, padded):
    cosine, sine = trig_tables(cells)
    split = cells // 2
    x_rows = np.zeros((2 * padded, cells), np.float32)
    x_rows[:half] = cosine[:half]
    x_rows[padded : padded + half] = -sine[:half]
    x_swapped = np.concatenate([x_rows[:, split:], x_rows[:, :split]], axis=1)
    y_rows = np.concatenate([cosine, -sine], axis=0)
    forward = (
        np.stack([x_rows, x_swapped]),
        np.stack([y_rows, y_rows[:, ::-1]]),
        np.stack([lane_mixes(cosine, -sine), lane_mixes(cosine[::-1], -sine[::-1])]),
    )
    twice = np.full((half,), 2.0, np.float32)
    twice[0] = 1.0
    twice[-1] = 1.0
    x_back = np.zeros((cells, 2 * padded), np.float32)
    x_back[:, :half] = cosine[:, :half] * twice
    x_back[:, padded : padded + half] = -sine[:, :half] * twice
    backward = (
        x_back,
        np.concatenate([cosine, sine], axis=0),
        lane_mixes(cosine, sine),
    )
    return (
        tuple(jnp.asarray(table, BF16) for table in forward),
        tuple(jnp.asarray(table, BF16) for table in backward),
    )


def group_of(half):
    return max(size for size in range(1, 12) if half % size == 0)


def plane_transform(tiles, y_rows, mixes):
    cells, lanes = tiles[0].shape
    mixed = jnp.dot(y_rows, jnp.concatenate(tiles, axis=1), preferred_element_type=F32)
    mixed = mixed.astype(BF16)
    parts = [mixed[:, n * lanes : (n + 1) * lanes] for n in range(len(tiles))]
    real = jnp.concatenate([part[:cells] for part in parts], axis=0)
    imag = jnp.concatenate([part[cells:] for part in parts], axis=0)
    return jnp.dot(
        jnp.concatenate([real, imag], axis=1), mixes, preferred_element_type=F32
    )


def forward_kernel(
    half, padded, rotated, core, turns, own, received, x_rows, y_rows, mixes, *refs
):
    out, tiles = refs[-2:]
    cells = y_rows.shape[2]
    lanes = 2 * cells
    group = group_of(half)
    grid = jnp.concatenate([own[0, 0].astype(F32).astype(BF16), received[0]], axis=0)
    low = lax.broadcasted_iota(jnp.int32, (padded, lanes), 1) < cells
    wide = 8 * lanes
    for block in range(cells * cells // wide):
        rows = jnp.dot(
            x_rows[0], grid[:, block * wide : (block + 1) * wide], preferred_element_type=F32
        )
        for piece in range(wide // lanes):
            real = rows[:padded, piece * lanes : (piece + 1) * lanes]
            imag = rows[padded:, piece * lanes : (piece + 1) * lanes]
            y = 2 * (block * (wide // lanes) + piece)
            tiles[pl.ds(y, padded, stride=cells), :] = jnp.where(
                low, real, pltpu.roll(imag, cells, 1)
            )
            tiles[pl.ds(y + 1, padded, stride=cells), :] = jnp.where(
                low, pltpu.roll(real, cells, 1), imag
            )

    def tile_at(k):
        return pl.ds(pl.multiple_of(k * cells, cells), cells)

    if rotated:

        @pl.when(turns[0] % 2 == 1)
        def _():
            def turn(step, carry):
                for n in range(group):
                    where = tile_at(step * group + n)
                    turned = jnp.transpose(tiles[where, :])
                    tiles[where, :] = jnp.concatenate([turned[:cells], turned[cells:]], axis=1)
                return carry

            lax.fori_loop(0, half // group, turn, 0)

    def body(step, carry):
        loaded = [tiles[tile_at(step * group + n), :].astype(BF16) for n in range(group)]
        done = plane_transform(loaded, y_rows[0], mixes[0])
        out[pl.ds(step * group, group)] = done.astype(BF16).reshape(group, cells, lanes)
        return carry

    lax.fori_loop(0, half // group, body, 0)


def forward(occupancy, received, core, turns, tables, half, padded, rotated, channel, after):
    mine, thickness, plane = received.shape
    cells = tables[1].shape[2]
    lanes = 2 * cells

    def y_reversed(turns):
        return (((turns[0] + 1) % 4) // 2 if rotated else 0, 0, 0)

    def z_reversed(turns):
        return (turns[0] // 2 if rotated else 0, 0, 0)

    grid_spec = pltpu.PrefetchScalarGridSpec(
        num_scalar_prefetch=2,
        grid=(1,),
        in_specs=[
            pl.BlockSpec((1, 1, thickness, plane), lambda c, f, t: (0, f[0] * mine + channel, 0, 0)),
            pl.BlockSpec((1, thickness, plane), lambda c, f, t: (channel, 0, 0)),
            pl.BlockSpec((1, 2 * padded, cells), lambda c, f, t: (f[0], 0, 0)),
            pl.BlockSpec((1, lanes, cells), lambda c, f, t: y_reversed(t)),
            pl.BlockSpec((1, 2 * lanes, lanes), lambda c, f, t: z_reversed(t)),
        ]
        + [pl.BlockSpec(memory_space=pl.ANY)] * len(after),
        out_specs=pl.BlockSpec((half, cells, lanes), lambda c, f, t: (0, 0, 0)),
        scratch_shapes=[pltpu.VMEM((padded * cells, lanes), F32)],
    )
    return pl.pallas_call(
        lambda *refs: forward_kernel(half, padded, rotated, *refs),
        out_shape=jax.ShapeDtypeStruct((half, cells, lanes), BF16),
        grid_spec=grid_spec,
        name="forward_pose" if rotated else "forward_receptor",
        compiler_params=pltpu.CompilerParams(vmem_limit_bytes=VMEM_BYTES),
        cost_estimate=pl.CostEstimate(
            flops=half * 6 * lanes * lanes * cells,
            bytes_accessed=plane * thickness * 20,
            transcendentals=0,
        ),
    )(core, turns, occupancy, received, *tables, *after)


def partial_cross(scales, receptors, ligands, where, cells):
    same = None
    swapped = None
    for scale, receptor, ligand in zip(scales, receptors, ligands):
        left = receptor[where].astype(F32) * scale
        right = ligand(where).astype(F32)
        turned = pltpu.roll(right, cells, right.ndim - 1)
        same = left * right if same is None else same + left * right
        swapped = left * turned if swapped is None else swapped + left * turned
    axis = same.ndim - 1
    low = lax.broadcasted_iota(jnp.int32, same.shape, axis) < cells
    real = same + pltpu.roll(same, cells, axis)
    imag = swapped - pltpu.roll(swapped, cells, axis)
    return jnp.where(low, real, imag)


def chosen(pick_second, first, second):
    return lambda where: jnp.where(pick_second, second[where], first[where])


def cross_kernel(mine, keep, core, weights, *refs):
    receptors, firsts, seconds = refs[:mine], refs[mine : 2 * mine], refs[2 * mine : 3 * mine]
    out = refs[-1]
    group, cells, _ = out.shape
    volume = 1.0 / float(cells) ** 3
    scales = [weights[core[0] * mine + c] * volume for c in range(mine)]
    second = core[0] == int(keep)
    ligands = [chosen(second, *pair) for pair in zip(firsts, seconds)]

    for k in range(group):
        out[k] = partial_cross(scales, receptors, ligands, k, cells).astype(out.dtype)


def vmem():
    return pl.BlockSpec(memory_space=pltpu.VMEM)


def smem():
    return pl.BlockSpec(memory_space=pltpu.SMEM)


def cross_part(keep, core, weights, receptor, first, second, after):
    mine = len(receptor)
    half, cells, lanes = receptor[0].shape
    group = group_of(half)
    block = (group, cells, lanes)

    def used(is_second):
        def index(k, core):
            wanted = int(keep) if is_second else int(not keep)
            return (jnp.where(core[0] == wanted, k, 0), 0, 0)

        return pl.BlockSpec(block, index)

    grid_spec = pltpu.PrefetchScalarGridSpec(
        num_scalar_prefetch=1,
        grid=(half // group,),
        in_specs=[smem()]
        + [pl.BlockSpec(block, lambda k, core: (k, 0, 0))] * mine
        + [used(False)] * mine
        + [used(True)] * mine
        + [pl.BlockSpec(memory_space=pl.ANY)] * len(after),
        out_specs=pl.BlockSpec(block, lambda k, core: (k, 0, 0)),
    )
    return pl.pallas_call(
        lambda *refs: cross_kernel(mine, keep, *refs),
        out_shape=jax.ShapeDtypeStruct((half, cells, lanes), F32 if keep else BF16),
        grid_spec=grid_spec,
        name="cross_keep" if keep else "cross_send",
        compiler_params=pltpu.CompilerParams(vmem_limit_bytes=VMEM_BYTES),
        cost_estimate=pl.CostEstimate(
            flops=mine * half * cells * lanes * 10,
            bytes_accessed=half * cells * lanes * 14,
            transcendentals=0,
        ),
    )(core, weights, *receptor, *first, *second, *after)


def inverse_kernel(padded, kept, arrived, x_back, y_rows, mixes, *refs):
    out, tiles, lined = refs[-3:]
    half, cells, lanes = kept.shape
    group = group_of(half)
    tiles[half * cells :, :] = jnp.zeros(((padded - half) * cells, lanes), F32)
    row = lax.broadcasted_iota(jnp.int32, (cells, lanes), 0)
    lane = lax.broadcasted_iota(jnp.int32, (cells, lanes), 1) % cells
    origin = row + lane

    def body(step, carry):
        loaded = []
        for n in range(group):
            k = step * group + n
            cross = kept[k] + arrived[k].astype(F32)
            if n == 0:
                cross = jnp.where(origin + k > 0, cross, 0.0)
            loaded.append(cross.astype(BF16))
        done = plane_transform(loaded, y_rows[...], mixes[...])
        size = group * cells
        tiles[pl.ds(pl.multiple_of(step * size, size), size), :] = done
        return carry

    lax.fori_loop(0, half // group, body, 0)
    low = lax.broadcasted_iota(jnp.int32, (padded, lanes), 1) < cells
    for y in range(0, cells, 2):
        even = tiles[pl.ds(y, padded, stride=cells), :]
        odd = tiles[pl.ds(y + 1, padded, stride=cells), :]
        where = slice(y * cells, y * cells + lanes)
        real = jnp.where(low, even, pltpu.roll(odd, cells, 1))
        imag = jnp.where(low, pltpu.roll(even, cells, 1), odd)
        lined[:, where] = jnp.concatenate([real, imag], axis=0).astype(BF16)
    best = None
    wide = 8 * lanes
    for block in range(cells * cells // wide):
        scores = jnp.dot(
            x_back[...], lined[:, block * wide : (block + 1) * wide], preferred_element_type=F32
        )
        for piece in range(wide // lanes):
            part = scores[:, piece * lanes : (piece + 1) * lanes]
            best = part if best is None else jnp.maximum(best, part)
    top = jnp.max(jnp.transpose(best), axis=0, keepdims=True)
    out[...] = top * (1.0 / (cells * math.sqrt(cells)))


def inverse(kept, arrived, tables, padded, after):
    half, cells, lanes = kept.shape
    return pl.pallas_call(
        lambda *refs: inverse_kernel(padded, *refs),
        out_shape=jax.ShapeDtypeStruct((1, cells), F32),
        in_specs=[vmem()] * 5 + [pl.BlockSpec(memory_space=pl.ANY)] * len(after),
        out_specs=vmem(),
        scratch_shapes=[
            pltpu.VMEM((padded * cells, lanes), F32),
            pltpu.VMEM((2 * padded, cells * cells), BF16),
        ],
        name="inverse_pair",
        compiler_params=pltpu.CompilerParams(vmem_limit_bytes=VMEM_BYTES),
        cost_estimate=pl.CostEstimate(
            flops=half * 6 * lanes * lanes * cells,
            bytes_accessed=half * cells * lanes * 16,
            transcendentals=0,
        ),
    )(kept, arrived, *tables, *after)


def shards(receptor_occupancy, ligand_occupancy, rot_index, receptor_extent, channel_weight):
    channels = receptor_occupancy.shape[1]
    thickness = receptor_occupancy.shape[2]
    parts = lax.axis_size("fft")
    if parts != LIG_STEPS or channels % parts:
        raise ValueError("unsupported split")
    mine = channels // parts
    cells = thickness * parts
    half = cells // 2 + 1
    padded = -(-half // 8) * 8
    me = lax.axis_index("fft").astype(jnp.int32)
    forward_tables, backward_tables = make_tables(cells, half, padded)
    core = me[None]

    def other_channels(occupancy):
        theirs = lax.dynamic_slice_in_dim(occupancy[0], (1 - me) * mine, mine, 0)
        return passed_along(theirs.astype(BF16), "fft", 1)

    extents = [receptor_extent]
    for steps in range(1, REC_STEPS):
        extents.append(passed_along(receptor_extent, "rec", steps))
    receptor_in = other_channels(receptor_occupancy)
    ligand_in = other_channels(ligand_occupancy)

    def hopped(value, axis):
        return passed_along(value, axis, 1)

    def spectrum(rotated, channel, after):
        occupancy, received = (
            (ligand_occupancy, ligand_in) if rotated else (receptor_occupancy, receptor_in)
        )
        return forward(
            occupancy, received, core, rot_index, forward_tables, half, padded, rotated,
            channel, after,
        )

    receptor = [spectrum(False, 0, [])]
    first = []
    for channel in range(mine):
        first.append(spectrum(True, channel, [*receptor, *first][-1:]))
    for channel in range(1, mine):
        receptor.append(spectrum(False, channel, [*first, *receptor[1:]][-1:]))
    receptors = [receptor]
    for _ in range(1, REC_STEPS):
        receptors.append([hopped(each, "rec") for each in receptors[-1]])
    second = [hopped(each, "lig") for each in first]

    def crossed(keep, step, after):
        return cross_part(keep, core, channel_weight, receptors[step], first, second, after)

    tops = [None] * REC_STEPS
    pending = []
    last = []
    for step in (1, 0, *range(2, REC_STEPS)):
        sent = crossed(False, step, last)
        arrived = passed_along(sent, "fft", 1)
        kept = crossed(True, step, [sent])
        pending.append((step, kept, arrived))
        last = [kept]
        if step == 1:
            continue
        while pending:
            place, kept, arrived = pending.pop(0)
            tops[place] = inverse(kept, arrived, backward_tables, padded, last)
            last = [tops[place]]
    ours = jnp.concatenate(tops, axis=0)
    theirs = passed_along(ours, "fft", 1)
    start = me * thickness
    ours = lax.dynamic_slice_in_dim(ours, start, thickness, 1)
    theirs = lax.dynamic_slice_in_dim(theirs, start, thickness, 1)
    steps = jnp.arange(LIG_STEPS, dtype=jnp.int32)[None, :, None]
    both = jnp.where(steps == me, ours[:, None], theirs[:, None])
    planes = start + jnp.arange(thickness, dtype=jnp.int32)
    limit = jnp.concatenate(extents)[:, None, None]
    return jnp.where(planes[None, None, :] < limit, both, 0.0)[None]


def solution(mesh):
    placed = (
        P(("groups", "rec", "lig"), None, "fft", None),
        P(("groups", "rec", "lig"), None, "fft", None),
        P(("groups", "rec", "lig")),
        P(("groups", "rec", "lig")),
        P(),
    )

    return jax.shard_map(
        shards,
        mesh=mesh,
        in_specs=placed,
        out_specs=P(("groups", "rec", "lig"), None, None, "fft"),
        check_vma=False,
    )
```

profile of v0, /device:TPU:0, one launch (start us, length us, event | category | flops | bytes accessed | tf_op | source)
XLA Modules:
  0.0 99.5 jit_solution(9042232187644325082)
XLA Ops:
  0.0 1.4 %fusion = bf16[2,32,4096]{2,1,0:T(8,128)(2,1)S(1)} fusion(s32[1,4,32,4096]{3,2,1,0:T(8,128)} %refs_2_.10, s32[]{:T(128)S(6)} %select_n.30), kind=kLoop, calls=%fused_computation.2 | loop fusion | flops 262144 | bytes 1572868 | tf_op jit(solution)/shard_map/convert_element_type | solution.py:332
  1.4 0.0 copy-start
  1.5 0.6 collective-permute-start.2
  2.0 1.3 %fusion.1 = bf16[2,32,4096]{2,1,0:T(8,128)(2,1)S(1)} fusion(s32[1,4,32,4096]{3,2,1,0:T(8,128)} %refs_2_.9, s32[]{:T(128)S(6)} %select_n.30), kind=kLoop, calls=%fused_computation.3 | loop fusion | flops 262144 | bytes 1572868 | tf_op jit(solution)/shard_map/convert_element_type | solution.py:332
  3.4 0.2 collective-permute-start.3
  4.2 0.0 collective-permute-done.2.refs_3_
  4.2 0.0 copy-done.8
  4.2 0.0 copy-done.7
  4.2 0.0 copy-done.6
  4.2 0.0 copy-done.1
  4.2 2.5 %forward_receptor.2.refs_7_.refs_2_ = bf16[33,64,128]{2,1,0:T(8,128)(2,1)S(1)} custom-call(s32[1]{0:T(128)} %bitcast.refs_0_, s32[1]{0:T(128)S(6)} %copy.12.refs_1_, s32[1,4,32,4096]{3,2,1,0:T(8,128)S(1)} %copy-done.1, bf16[2,32,4096]{2,1,0:T(8,128)(2,1)S(1)} %collective-permute-done.2.refs_3_, bf16[2,80,64]{2,1,0:T(8,128)(2,1)S(1)} %copy-done.8, ...), custom_call_target="tpu_custom_call" | custom-call | flops 207618048 | bytes 2621440 | tf_op jit(solution)/shard_map/forward_receptor/pallas_call | solution.py:159
  6.8 0.0 copy-start.2
  6.8 0.0 collective-permute-done.3.refs_3_
  6.8 0.0 copy-done
  6.8 3.7 %forward_pose.2.refs_7_.refs_4_ = bf16[33,64,128]{2,1,0:T(8,128)(2,1)S(1)} custom-call(s32[1]{0:T(128)} %bitcast.refs_0_, s32[1]{0:T(128)S(6)} %copy.12.refs_1_, s32[1,4,32,4096]{3,2,1,0:T(8,128)S(1)} %copy-done, bf16[2,32,4096]{2,1,0:T(8,128)(2,1)S(1)} %collective-permute-done.3.refs_3_, bf16[2,80,64]{2,1,0:T(8,128)(2,1)S(1)} %copy-done.8, ...), custom_call_target="tpu_custom_call" | custom-call | flops 207618048 | bytes 2621440 | tf_op jit(solution)/shard_map/forward_pose/pallas_call | solution.py:159
  10.5 3.7 %forward_pose.3.refs_7_.refs_5_ = bf16[33,64,128]{2,1,0:T(8,128)(2,1)S(1)} custom-call(s32[1]{0:T(128)} %bitcast.refs_0_, s32[1]{0:T(128)S(6)} %copy.12.refs_1_, s32[1,4,32,4096]{3,2,1,0:T(8,128)S(1)} %copy-done, bf16[2,32,4096]{2,1,0:T(8,128)(2,1)S(1)} %collective-permute-done.3.refs_3_, bf16[2,80,64]{2,1,0:T(8,128)(2,1)S(1)} %copy-done.8, ...), custom_call_target="tpu_custom_call" | custom-call | flops 207618048 | bytes 2621440 | tf_op jit(solution)/shard_map/forward_pose/pallas_call | solution.py:159
  14.2 0.0 copy-start.12
  14.2 2.5 %forward_receptor.3.refs_3_ = bf16[33,64,128]{2,1,0:T(8,128)(2,1)S(1)} custom-call(s32[1]{0:T(128)} %bitcast.refs_0_, s32[1]{0:T(128)S(6)} %copy.12.refs_1_, s32[1,4,32,4096]{3,2,1,0:T(8,128)S(1)} %copy-done.1, bf16[2,32,4096]{2,1,0:T(8,128)(2,1)S(1)} %collective-permute-done.2.refs_3_, bf16[2,80,64]{2,1,0:T(8,128)(2,1)S(1)} %copy-done.8, ...), custom_call_target="tpu_custom_call" | custom-call | flops 207618048 | bytes 2621440 | tf_op jit(solution)/shard_map/forward_receptor/pallas_call | solution.py:159
  16.7 0.0 copy-start.4
  16.8 3.0 %collective-permute-start.7 = (bf16[33,64,128]{2,1,0:T(8,128)(2,1)S(1)}, bf16[33,64,128]{2,1,0:T(8,128)(2,1)}, u32[]{:S(2)}, u32[]{:S(2)}) collective-permute-start(bf16[33,64,128]{2,1,0:T(8,128)(2,1)S(1)} %forward_receptor.3.refs_3_), channel_id=1, source_target_pairs={{0,4},{4,8},{8,12},{12,0},{1,5},{5,9},{9,13},{13,1},{2,6},{6,10},{... | collective-permute-start | bytes 1622024 | tf_op jit(solution)/shard_map/ppermute | solution.py:22
  19.7 0.0 collective-permute-start.5
  19.7 2.0 %collective-permute-start.4 = (bf16[33,64,128]{2,1,0:T(8,128)(2,1)S(1)}, bf16[33,64,128]{2,1,0:T(8,128)(2,1)S(1)}, u32[]{:S(2)}, u32[]{:S(2)}) collective-permute-start(bf16[33,64,128]{2,1,0:T(8,128)(2,1)S(1)} %forward_pose.2.refs_7_.refs_4_), channel_id=1, source_target_pairs={{0,2},{2,0},{1,3},{3,1},{4,6},{6,4},{5,7},{7,5},{8,10},{10,8},{9,1... | collective-permute-start | bytes 1622024 | tf_op jit(solution)/shard_map/ppermute | solution.py:22
  21.8 0.1 collective-permute-start.6
  21.8 13.2 %collective-permute-done.7.refs_3_ = bf16[33,64,128]{2,1,0:T(8,128)(2,1)} collective-permute-done((bf16[33,64,128]{2,1,0:T(8,128)(2,1)S(1)}, bf16[33,64,128]{2,1,0:T(8,128)(2,1)}, u32[]{:S(2)}, u32[]{:S(2)}) %collective-permute-start.7) | collective-permute-done | bytes 540704 | tf_op jit(solution)/shard_map/ppermute | solution.py:22
  35.0 0.0 collective-permute-done.5.refs_7_
  35.0 10.4 %collective-permute-done.4.refs_6_ = bf16[33,64,128]{2,1,0:T(8,128)(2,1)S(1)} collective-permute-done((bf16[33,64,128]{2,1,0:T(8,128)(2,1)S(1)}, bf16[33,64,128]{2,1,0:T(8,128)(2,1)S(1)}, u32[]{:S(2)}, u32[]{:S(2)}) %collective-permute-start.4) | collective-permute-done | bytes 540704 | tf_op jit(solution)/shard_map/ppermute | solution.py:22
  45.4 0.7 collective-permute-done.6.refs_2_
  46.0 0.0 copy-done.12
  46.0 4.4 %cross_send.3.refs_8_ = bf16[33,64,128]{2,1,0:T(8,128)(2,1)} custom-call(s32[1]{0:T(128)} %bitcast.refs_0_, f32[4]{0:T(128)S(1)} %copy-done.12, bf16[33,64,128]{2,1,0:T(8,128)(2,1)} %collective-permute-done.6.refs_2_, bf16[33,64,128]{2,1,0:T(8,128)(2,1)} %collective-permute-done.7.refs_3_, bf16[33,64,128]{2,1,0:T(8,128)(2,1)S(1)} %forward_pose.2.refs_7_.refs_4_, ...), custom_call_target="tpu_custom_call" | custom-call | flops 5406720 | bytes 3784704 | tf_op jit(solution)/shard_map/cross_send/pallas_call | solution.py:237
  50.4 0.0 collective-permute-start.9
  50.4 3.6 %cross_keep.3.refs_8_.refs_0_ = f32[33,64,128]{2,1,0:T(8,128)S(1)} custom-call(s32[1]{0:T(128)} %bitcast.refs_0_, f32[4]{0:T(128)S(1)} %copy-done.12, bf16[33,64,128]{2,1,0:T(8,128)(2,1)} %collective-permute-done.6.refs_2_, bf16[33,64,128]{2,1,0:T(8,128)(2,1)} %collective-permute-done.7.refs_3_, bf16[33,64,128]{2,1,0:T(8,128)(2,1)S(1)} %forward_pose.2.refs_7_.refs_4_, ...), custom_call_target="tpu_custom_call" | custom-call | flops 5406720 | bytes 3784704 | tf_op jit(solution)/shard_map/cross_keep/pallas_call | solution.py:237
  54.0 0.0 copy-done.2
  54.0 0.0 copy-done.4
  54.1 3.7 %cross_send.4.refs_8_ = bf16[33,64,128]{2,1,0:T(8,128)(2,1)} custom-call(s32[1]{0:T(128)} %bitcast.refs_0_, f32[4]{0:T(128)S(1)} %copy-done.12, bf16[33,64,128]{2,1,0:T(8,128)(2,1)S(1)} %forward_receptor.2.refs_7_.refs_2_, bf16[33,64,128]{2,1,0:T(8,128)(2,1)S(1)} %forward_receptor.3.refs_3_, bf16[33,64,128]{2,1,0:T(8,128)(2,1)S(1)} %forward_pose.2.refs_7_.refs_4_, ...), custom_call_target="tpu_custom_call" | custom-call | flops 5406720 | bytes 3784704 | tf_op jit(solution)/shard_map/cross_send/pallas_call | solution.py:237
  57.7 0.5 collective-permute-start.8
  58.2 0.0 collective-permute-start.11
  58.2 2.5 %collective-permute-start.10 = (bf16[33,64,128]{2,1,0:T(8,128)(2,1)}, bf16[33,64,128]{2,1,0:T(8,128)(2,1)}, u32[]{:S(2)}, u32[]{:S(2)}) collective-permute-start(bf16[33,64,128]{2,1,0:T(8,128)(2,1)} %collective-permute-done.6.refs_2_), channel_id=1, source_target_pairs={{0,4},{4,8},{8,12},{12,0},{1,5},{5,9},{9,13},{13,1},{2,6},{6,10},{... | collective-permute-start | bytes 1622024 | tf_op jit(solution)/shard_map/ppermute | solution.py:22
  60.7 0.4 collective-permute-start
  61.8 0.0 copy-start.3
  61.8 1.0 %copy-done.3 = bf16[33,64,128]{2,1,0:T(8,128)(2,1)S(1)} copy-done((bf16[33,64,128]{2,1,0:T(8,128)(2,1)S(1)}, bf16[33,64,128]{2,1,0:T(8,128)(2,1)}, u32[]{:S(2)}) %copy-start.3) | copy-done | bytes 540696
  62.8 1.0 %copy-done.5 = bf16[33,64,128]{2,1,0:T(8,128)(2,1)S(1)} copy-done((bf16[33,64,128]{2,1,0:T(8,128)(2,1)S(1)}, bf16[33,64,128]{2,1,0:T(8,128)(2,1)}, u32[]{:S(2)}) %copy-start.5) | copy-done | bytes 540696
  63.9 2.9 %cross_keep.4.refs_5_.refs_0_ = f32[33,64,128]{2,1,0:T(8,128)S(1)} custom-call(s32[1]{0:T(128)} %bitcast.refs_0_, f32[4]{0:T(128)S(1)} %copy-done.12, bf16[33,64,128]{2,1,0:T(8,128)(2,1)S(1)} %copy-done.3, bf16[33,64,128]{2,1,0:T(8,128)(2,1)S(1)} %copy-done.5, bf16[33,64,128]{2,1,0:T(8,128)(2,1)S(1)} %forward_pose.2.refs_7_.refs_4_, ...), custom_call_target="tpu_custom_call" | custom-call | flops 5406720 | bytes 3784704 | tf_op jit(solution)/shard_map/cross_keep/pallas_call | solution.py:237
  66.8 0.0 collective-permute-done.9.refs_1_
  66.8 1.6 %collective-permute-start.1 = (s32[1]{0:T(128)}, s32[1]{0:T(128)}, u32[]{:S(2)}, u32[]{:S(2)}) collective-permute-start(s32[1]{0:T(128)} %param.14), channel_id=1, source_target_pairs={{0,8},{4,12},{8,0},{12,4},{1,9},{5,13},{9,1},{13,5},{2,10},{6,14},... | collective-permute-start | bytes 20 | tf_op jit(solution)/shard_map/ppermute | solution.py:22
  68.4 0.0 copy-done.9
  68.4 3.5 %inverse_pair.3.refs_5_ = f32[1,64]{1,0:T(1,128)S(1)} custom-call(f32[33,64,128]{2,1,0:T(8,128)S(1)} %cross_keep.3.refs_8_.refs_0_, bf16[33,64,128]{2,1,0:T(8,128)(2,1)} %collective-permute-done.9.refs_1_, bf16[64,80]{1,0:T(8,128)(2,1)S(1)} %copy-done.11, bf16[128,64]{1,0:T(8,128)(2,1)S(1)} %copy-done.10, bf16[256,128]{1,0:T(8,128)(2,1)S(1)} %copy-done.9, ...), custom_call_target="tpu_custom_call" | custom-call | flops 207618048 | bytes 4325376 | tf_op jit(solution)/shard_map/inverse_pair/pallas_call | solution.py:297
  71.9 0.0 collective-permute-done.8.refs_1_
  72.0 3.5 %inverse_pair.4.refs_8_ = f32[1,64]{1,0:T(1,128)S(1)} custom-call(f32[33,64,128]{2,1,0:T(8,128)S(1)} %cross_keep.4.refs_5_.refs_0_, bf16[33,64,128]{2,1,0:T(8,128)(2,1)} %collective-permute-done.8.refs_1_, bf16[64,80]{1,0:T(8,128)(2,1)S(1)} %copy-done.11, bf16[128,64]{1,0:T(8,128)(2,1)S(1)} %copy-done.10, bf16[256,128]{1,0:T(8,128)(2,1)S(1)} %copy-done.9, ...), custom_call_target="tpu_custom_call" | custom-call | flops 207618048 | bytes 4325376 | tf_op jit(solution)/shard_map/inverse_pair/pallas_call | solution.py:297
  75.5 0.0 collective-permute-done.11.refs_3_
  75.5 10.6 %collective-permute-done.10.refs_2_ = bf16[33,64,128]{2,1,0:T(8,128)(2,1)} collective-permute-done((bf16[33,64,128]{2,1,0:T(8,128)(2,1)}, bf16[33,64,128]{2,1,0:T(8,128)(2,1)}, u32[]{:S(2)}, u32[]{:S(2)}) %collective-permute-start.10) | collective-permute-done | bytes 540704 | tf_op jit(solution)/shard_map/ppermute | solution.py:22
  86.1 3.6 %cross_send.5.refs_8_ = bf16[33,64,128]{2,1,0:T(8,128)(2,1)S(1)} custom-call(s32[1]{0:T(128)} %bitcast.refs_0_, f32[4]{0:T(128)S(1)} %copy-done.12, bf16[33,64,128]{2,1,0:T(8,128)(2,1)} %collective-permute-done.10.refs_2_, bf16[33,64,128]{2,1,0:T(8,128)(2,1)} %collective-permute-done.11.refs_3_, bf16[33,64,128]{2,1,0:T(8,128)(2,1)S(1)} %forward_pose.2.refs_7_.refs_4_, ...), custom_call_target="tpu_custom_call" | custom-call | flops 5406720 | bytes 3784704 | tf_op jit(solution)/shard_map/cross_send/pallas_call | solution.py:237
  89.8 0.1 collective-permute-start.12
  89.9 0.0 collective-permute-done
  89.9 0.0 collective-permute-done.1
  89.9 1.3 %pad_add_fusion = s32[3]{0:T(128)S(1)} fusion(s32[1]{0:T(128)} %collective-permute-done.1, s32[1]{0:T(128)} %collective-permute-done, s32[1]{0:T(128)S(6)} %copy.13), kind=kLoop, calls=%fused_computation.9 | loop fusion | flops 6 | bytes 24 | tf_op jit(solution)/shard_map/concatenate | solution.py:389
  91.2 0.1 broadcast_compare_fusion
  91.3 3.6 %cross_keep.5.refs_0_.refs_5_ = f32[33,64,128]{2,1,0:T(8,128)S(1)} custom-call(s32[1]{0:T(128)} %bitcast.refs_0_, f32[4]{0:T(128)S(1)} %copy-done.12, bf16[33,64,128]{2,1,0:T(8,128)(2,1)} %collective-permute-done.10.refs_2_, bf16[33,64,128]{2,1,0:T(8,128)(2,1)} %collective-permute-done.11.refs_3_, bf16[33,64,128]{2,1,0:T(8,128)(2,1)S(1)} %forward_pose.2.refs_7_.refs_4_, ...), custom_call_target="tpu_custom_call" | custom-call | flops 5406720 | bytes 3784704 | tf_op jit(solution)/shard_map/cross_keep/pallas_call | solution.py:237
  94.9 0.0 collective-permute-done.12.refs_1_
  94.9 2.5 %inverse_pair.5 = f32[1,64]{1,0:T(1,128)S(1)} custom-call(f32[33,64,128]{2,1,0:T(8,128)S(1)} %cross_keep.5.refs_0_.refs_5_, bf16[33,64,128]{2,1,0:T(8,128)(2,1)S(1)} %collective-permute-done.12.refs_1_, bf16[64,80]{1,0:T(8,128)(2,1)S(1)} %copy-done.11, bf16[128,64]{1,0:T(8,128)(2,1)S(1)} %copy-done.10, bf16[256,128]{1,0:T(8,128)(2,1)S(1)} %copy-done.9, ...), custom_call_target="tpu_custom_call" | custom-call | flops 207618048 | bytes 4325376 | tf_op jit(solution)/shard_map/inverse_pair/pallas_call | solution.py:297
  97.4 0.5 collective-permute-start.13
  98.0 0.1 constant_dynamic-slice_fusion.1
  98.0 0.7 collective-permute-done.13
  98.8 0.1 constant_dynamic-slice_fusion
  98.9 0.7 select_select_fusion
  (13 shorter events, 0.0 us)
Async XLA Ops:
  0.0 4.2 %copy-start.8 = (bf16[2,80,64]{2,1,0:T(8,128)(2,1)S(1)}, bf16[2,80,64]{2,1,0:T(8,128)(2,1)}, u32[]{:S(2)}) copy-start(bf16[2,80,64]{2,1,0:T(8,128)(2,1)} %constant.32.clone.refs_4_) | copy-start | bytes 61444
  0.0 4.2 %copy-start.7 = (bf16[2,128,64]{2,1,0:T(8,128)(2,1)S(1)}, bf16[2,128,64]{2,1,0:T(8,128)(2,1)}, u32[]{:S(2)}) copy-start(bf16[2,128,64]{2,1,0:T(8,128)(2,1)} %constant.33.clone.refs_5_) | copy-start | bytes 98308
  0.0 4.2 %copy-start.6 = (bf16[2,256,128]{2,1,0:T(8,128)(2,1)S(1)}, bf16[2,256,128]{2,1,0:T(8,128)(2,1)}, u32[]{:S(2)}) copy-start(bf16[2,256,128]{2,1,0:T(8,128)(2,1)} %constant.34.clone.refs_6_) | copy-start | bytes 393220
  0.0 4.2 %copy-start.1 = (s32[1,4,32,4096]{3,2,1,0:T(8,128)S(1)}, s32[1,4,32,4096]{3,2,1,0:T(8,128)}, u32[]{:S(2)}) copy-start(s32[1,4,32,4096]{3,2,1,0:T(8,128)} %refs_2_.10) | copy-start | bytes 6291460
  1.4 5.4 %copy-start = (s32[1,4,32,4096]{3,2,1,0:T(8,128)S(1)}, s32[1,4,32,4096]{3,2,1,0:T(8,128)}, u32[]{:S(2)}) copy-start(s32[1,4,32,4096]{3,2,1,0:T(8,128)} %refs_2_.9) | copy-start | bytes 6291460
  1.5 2.7 %collective-permute-start.2 = (bf16[2,32,4096]{2,1,0:T(8,128)(2,1)S(1)}, bf16[2,32,4096]{2,1,0:T(8,128)(2,1)S(1)}, u32[]{:S(2)}, u32[]{:S(2)}) collective-permute-start(bf16[2,32,4096]{2,1,0:T(8,128)(2,1)S(1)} %fusion), channel_id=1, source_target_pairs={{0,1},{1,0},{2,3},{3,2},{4,5},{5,4},{6,7},{7,6},{8,9},{9,8},{10,11... | collective-permute-start | bytes 1572872 | tf_op jit(solution)/shard_map/ppermute | solution.py:22
  3.4 3.4 %collective-permute-start.3 = (bf16[2,32,4096]{2,1,0:T(8,128)(2,1)S(1)}, bf16[2,32,4096]{2,1,0:T(8,128)(2,1)S(1)}, u32[]{:S(2)}, u32[]{:S(2)}) collective-permute-start(bf16[2,32,4096]{2,1,0:T(8,128)(2,1)S(1)} %fusion.1), channel_id=1, source_target_pairs={{0,1},{1,0},{2,3},{3,2},{4,5},{5,4},{6,7},{7,6},{8,9},{9,8},{10,11... | collective-permute-start | bytes 1572872 | tf_op jit(solution)/shard_map/ppermute | solution.py:22
  6.8 47.3 %copy-start.2 = (bf16[33,64,128]{2,1,0:T(8,128)(2,1)}, bf16[33,64,128]{2,1,0:T(8,128)(2,1)S(1)}, u32[]{:S(2)}) copy-start(bf16[33,64,128]{2,1,0:T(8,128)(2,1)S(1)} %forward_receptor.2.refs_7_.refs_2_) | copy-start | bytes 1622020
  14.2 31.9 %copy-start.12 = (f32[4]{0:T(128)S(1)}, f32[4]{0:T(128)}, u32[]{:S(2)}) copy-start(f32[4]{0:T(128)} %refs_1_.15) | copy-start | bytes 52
  16.7 37.3 %copy-start.4 = (bf16[33,64,128]{2,1,0:T(8,128)(2,1)}, bf16[33,64,128]{2,1,0:T(8,128)(2,1)S(1)}, u32[]{:S(2)}) copy-start(bf16[33,64,128]{2,1,0:T(8,128)(2,1)S(1)} %forward_receptor.3.refs_3_) | copy-start | bytes 1622020
  16.8 18.2 %collective-permute-start.7 = (bf16[33,64,128]{2,1,0:T(8,128)(2,1)S(1)}, bf16[33,64,128]{2,1,0:T(8,128)(2,1)}, u32[]{:S(2)}, u32[]{:S(2)}) collective-permute-start(bf16[33,64,128]{2,1,0:T(8,128)(2,1)S(1)} %forward_receptor.3.refs_3_), channel_id=1, source_target_pairs={{0,4},{4,8},{8,12},{12,0},{1,5},{5,9},{9,13},{13,1},{2,6},{6,10},{... | collective-permute-start | bytes 1622024 | tf_op jit(solution)/shard_map/ppermute | solution.py:22
  19.7 15.3 %collective-permute-start.5 = (bf16[33,64,128]{2,1,0:T(8,128)(2,1)S(1)}, bf16[33,64,128]{2,1,0:T(8,128)(2,1)S(1)}, u32[]{:S(2)}, u32[]{:S(2)}) collective-permute-start(bf16[33,64,128]{2,1,0:T(8,128)(2,1)S(1)} %forward_pose.3.refs_7_.refs_5_), channel_id=1, source_target_pairs={{0,2},{2,0},{1,3},{3,1},{4,6},{6,4},{5,7},{7,5},{8,10},{10,8},{9,1... | collective-permute-start | bytes 1622024 | tf_op jit(solution)/shard_map/ppermute | solution.py:22
  19.7 25.6 %collective-permute-start.4 = (bf16[33,64,128]{2,1,0:T(8,128)(2,1)S(1)}, bf16[33,64,128]{2,1,0:T(8,128)(2,1)S(1)}, u32[]{:S(2)}, u32[]{:S(2)}) collective-permute-start(bf16[33,64,128]{2,1,0:T(8,128)(2,1)S(1)} %forward_pose.2.refs_7_.refs_4_), channel_id=1, source_target_pairs={{0,2},{2,0},{1,3},{3,1},{4,6},{6,4},{5,7},{7,5},{8,10},{10,8},{9,1... | collective-permute-start | bytes 1622024 | tf_op jit(solution)/shard_map/ppermute | solution.py:22
  21.8 24.3 %collective-permute-start.6 = (bf16[33,64,128]{2,1,0:T(8,128)(2,1)S(1)}, bf16[33,64,128]{2,1,0:T(8,128)(2,1)}, u32[]{:S(2)}, u32[]{:S(2)}) collective-permute-start(bf16[33,64,128]{2,1,0:T(8,128)(2,1)S(1)} %forward_receptor.2.refs_7_.refs_2_), channel_id=1, source_target_pairs={{0,4},{4,8},{8,12},{12,0},{1,5},{5,9},{9,13},{13,1},{2,6},{6,10},{... | collective-permute-start | bytes 1622024 | tf_op jit(solution)/shard_map/ppermute | solution.py:22
  50.4 16.4 %collective-permute-start.9 = (bf16[33,64,128]{2,1,0:T(8,128)(2,1)}, bf16[33,64,128]{2,1,0:T(8,128)(2,1)}, u32[]{:S(2)}, u32[]{:S(2)}) collective-permute-start(bf16[33,64,128]{2,1,0:T(8,128)(2,1)} %cross_send.3.refs_8_), channel_id=1, source_target_pairs={{0,1},{1,0},{2,3},{3,2},{4,5},{5,4},{6,7},{7,6},{8,9},{9,8},{10,11... | collective-permute-start | bytes 1622024 | tf_op jit(solution)/shard_map/ppermute | solution.py:22
  57.7 14.2 %collective-permute-start.8 = (bf16[33,64,128]{2,1,0:T(8,128)(2,1)}, bf16[33,64,128]{2,1,0:T(8,128)(2,1)}, u32[]{:S(2)}, u32[]{:S(2)}) collective-permute-start(bf16[33,64,128]{2,1,0:T(8,128)(2,1)} %cross_send.4.refs_8_), channel_id=1, source_target_pairs={{0,1},{1,0},{2,3},{3,2},{4,5},{5,4},{6,7},{7,6},{8,9},{9,8},{10,11... | collective-permute-start | bytes 1622024 | tf_op jit(solution)/shard_map/ppermute | solution.py:22
  58.2 17.3 %collective-permute-start.11 = (bf16[33,64,128]{2,1,0:T(8,128)(2,1)}, bf16[33,64,128]{2,1,0:T(8,128)(2,1)}, u32[]{:S(2)}, u32[]{:S(2)}) collective-permute-start(bf16[33,64,128]{2,1,0:T(8,128)(2,1)} %collective-permute-done.7.refs_3_), channel_id=1, source_target_pairs={{0,4},{4,8},{8,12},{12,0},{1,5},{5,9},{9,13},{13,1},{2,6},{6,10},{... | collective-permute-start | bytes 1622024 | tf_op jit(solution)/shard_map/ppermute | solution.py:22
  58.2 27.9 %collective-permute-start.10 = (bf16[33,64,128]{2,1,0:T(8,128)(2,1)}, bf16[33,64,128]{2,1,0:T(8,128)(2,1)}, u32[]{:S(2)}, u32[]{:S(2)}) collective-permute-start(bf16[33,64,128]{2,1,0:T(8,128)(2,1)} %collective-permute-done.6.refs_2_), channel_id=1, source_target_pairs={{0,4},{4,8},{8,12},{12,0},{1,5},{5,9},{9,13},{13,1},{2,6},{6,10},{... | collective-permute-start | bytes 1622024 | tf_op jit(solution)/shard_map/ppermute | solution.py:22
  60.7 29.2 %collective-permute-start = (s32[1]{0:T(128)}, s32[1]{0:T(128)}, u32[]{:S(2)}, u32[]{:S(2)}) collective-permute-start(s32[1]{0:T(128)} %param.14), channel_id=1, source_target_pairs={{0,4},{4,8},{8,12},{12,0},{1,5},{5,9},{9,13},{13,1},{2,6},{6,10},{... | collective-permute-start | bytes 20 | tf_op jit(solution)/shard_map/ppermute | solution.py:22
  61.8 1.0 %copy-start.3 = (bf16[33,64,128]{2,1,0:T(8,128)(2,1)S(1)}, bf16[33,64,128]{2,1,0:T(8,128)(2,1)}, u32[]{:S(2)}) copy-start(bf16[33,64,128]{2,1,0:T(8,128)(2,1)} %copy-done.2) | copy-start | bytes 1622020
  62.8 1.0 %copy-start.5 = (bf16[33,64,128]{2,1,0:T(8,128)(2,1)S(1)}, bf16[33,64,128]{2,1,0:T(8,128)(2,1)}, u32[]{:S(2)}) copy-start(bf16[33,64,128]{2,1,0:T(8,128)(2,1)} %copy-done.4) | copy-start | bytes 1622020
  63.9 4.6 %copy-start.9 = (bf16[256,128]{1,0:T(8,128)(2,1)S(1)}, bf16[256,128]{1,0:T(8,128)(2,1)}, u32[]{:S(2)}) copy-start(bf16[256,128]{1,0:T(8,128)(2,1)} %constant.37.clone.refs_4_) | copy-start | bytes 196612
  63.9 4.6 %copy-start.10 = (bf16[128,64]{1,0:T(8,128)(2,1)S(1)}, bf16[128,64]{1,0:T(8,128)(2,1)}, u32[]{:S(2)}) copy-start(bf16[128,64]{1,0:T(8,128)(2,1)} %constant.36.clone.refs_3_) | copy-start | bytes 49156
  63.9 4.6 %copy-start.11 = (bf16[64,80]{1,0:T(8,128)(2,1)S(1)}, bf16[64,80]{1,0:T(8,128)(2,1)}, u32[]{:S(2)}) copy-start(bf16[64,80]{1,0:T(8,128)(2,1)} %constant.35.clone.refs_2_) | copy-start | bytes 30724
  66.8 23.1 %collective-permute-start.1 = (s32[1]{0:T(128)}, s32[1]{0:T(128)}, u32[]{:S(2)}, u32[]{:S(2)}) collective-permute-start(s32[1]{0:T(128)} %param.14), channel_id=1, source_target_pairs={{0,8},{4,12},{8,0},{12,4},{1,9},{5,13},{9,1},{13,5},{2,10},{6,14},... | collective-permute-start | bytes 20 | tf_op jit(solution)/shard_map/ppermute | solution.py:22
  89.8 5.2 %collective-permute-start.12 = (bf16[33,64,128]{2,1,0:T(8,128)(2,1)S(1)}, bf16[33,64,128]{2,1,0:T(8,128)(2,1)S(1)}, u32[]{:S(2)}, u32[]{:S(2)}) collective-permute-start(bf16[33,64,128]{2,1,0:T(8,128)(2,1)S(1)} %cross_send.5.refs_8_), channel_id=1, source_target_pairs={{0,1},{1,0},{2,3},{3,2},{4,5},{5,4},{6,7},{7,6},{8,9},{9,8},{10,11... | collective-permute-start | bytes 1622024 | tf_op jit(solution)/shard_map/ppermute | solution.py:22
  97.4 1.4 %collective-permute-start.13 = (f32[3,64]{1,0:T(4,128)S(1)}, f32[3,64]{1,0:T(4,128)S(1)}, u32[]{:S(2)}, u32[]{:S(2)}) collective-permute-start(f32[3,64]{1,0:T(4,128)S(1)} %pad_maximum_fusion), channel_id=1, source_target_pairs={{0,1},{1,0},{2,3},{3,2},{4,5},{5,4},{6,7},{7,6},{8,9},{9,8},{10,11... | collective-permute-start | bytes 2312 | tf_op jit(solution)/shard_map/ppermute | solution.py:22
where the time goes:
time: 100 us; the launch traced here: 99.5 us
  Pallas kernels  43.8 us (44%)
  waiting for transfers between devices  35.6 us (36%)
  starting transfers between devices  11.4 us (11%)
  other arithmetic  4.81 us (5%)
  local copies, waits for them, and re-layouts  2.28 us (2%)
  between operations  1.61 us (2%)
    ppermute x14, waiting for transfers between devices, passed_along(): return lax.ppermute(value, axis, pairs)  35.6 us
    pallas_call x6, Pallas kernels, cross_part(): pl.pallas_call(lambda *refs: cross_kernel(mine, keep, *refs), out_shape=j...  21.8 us
    pallas_call x4, Pallas kernels, forward(): pl.pallas_call(lambda *refs: forward_kernel(half, padded, rotated, *refs)...  12.5 us
    ppermute x14, starting transfers between devices, passed_along(): return lax.ppermute(value, axis, pairs)  11.4 us
    pallas_call x3, Pallas kernels, inverse(): pl.pallas_call(lambda *refs: inverse_kernel(padded, *refs), out_shape=jax...  9.48 us
    convert_element_type x2, other arithmetic, other_channels(): return passed_along(theirs.astype(BF16), 'fft', 1)  2.75 us
    unnamed x26, local copies, waits for them, and re-layouts  2.13 us
  transfers between devices with their start and end apart: 14, of which 5 were waited for; matrix products, arithmetic and copies ran while one was open for 3% of the time, Pallas kernels for 27%

commit v1 on v0

--- a/solution.py
+++ b/solution.py
@@ -313,6 +313,21 @@
     )(kept, arrived, *tables, *after)
 
 
+def marked(after):
+    def kernel(*refs):
+        refs[-1][...] = jnp.zeros_like(refs[-1])
+
+    return pl.pallas_call(
+        kernel,
+        out_shape=jax.ShapeDtypeStruct((8, 128), F32),
+        in_specs=[pl.BlockSpec(memory_space=pl.ANY)] * len(after),
+        out_specs=vmem(),
+        name="mark",
+        compiler_params=pltpu.CompilerParams(vmem_limit_bytes=VMEM_BYTES),
+        cost_estimate=pl.CostEstimate(flops=0, bytes_accessed=4096, transcendentals=0),
+    )(*after)
+
+
 def shards(receptor_occupancy, ligand_occupancy, rot_index, receptor_extent, channel_weight):
     channels = receptor_occupancy.shape[1]
     thickness = receptor_occupancy.shape[2]
@@ -349,23 +364,25 @@
             channel, after,
         )
 
-    receptor = [spectrum(False, 0, [])]
+    receptor = []
     first = []
     for channel in range(mine):
-        first.append(spectrum(True, channel, [*receptor, *first][-1:]))
-    for channel in range(1, mine):
-        receptor.append(spectrum(False, channel, [*first, *receptor[1:]][-1:]))
+        receptor.append(spectrum(False, channel, first[-1:]))
+        first.append(spectrum(True, channel, receptor[-1:]))
     receptors = [receptor]
     for _ in range(1, REC_STEPS):
         receptors.append([hopped(each, "rec") for each in receptors[-1]])
     second = [hopped(each, "lig") for each in first]
 
+    last = []
+    for each in receptors[1]:
+        last = [marked([each, *(last or first[-1:])])]
+
     def crossed(keep, step, after):
         return cross_part(keep, core, channel_weight, receptors[step], first, second, after)
 
     tops = [None] * REC_STEPS
     pending = []
-    last = []
     for step in (1, 0, *range(2, REC_STEPS)):
         sent = crossed(False, step, last)
         arrived = passed_along(sent, "fft", 1)

time: 100 us -> 101 us (1.010)
  starting transfers between devices: 11.4 us -> 13.5 us
  waiting for transfers between devices: 35.6 us -> 34.3 us
    ppermute x14, starting transfers between devices: 11.4 us -> 13.5 us  [passed_along(): return lax.ppermute(value, axis, pairs)]
    ppermute x14, waiting for transfers between devices: 35.6 us -> 34.3 us  [passed_along(): return lax.ppermute(value, axis, pairs)]
  transfers between devices with their start and end apart: 14 -> 14, of which waited for: 5 -> 6; matrix products, arithmetic and copies ran while one was open for 3% -> 3% of each run, Pallas kernels for 27% -> 37%
where the time goes in v1:
time: 101 us; the launch traced here: 100 us
  Pallas kernels  43.7 us (43%)
  waiting for transfers between devices  34.3 us (34%)
  starting transfers between devices  13.5 us (13%)
  other arithmetic  4.81 us (5%)
  local copies, waits for them, and re-layouts  2.28 us (2%)
  between operations  1.61 us (2%)
    ppermute x14, waiting for transfers between devices, passed_along(): return lax.ppermute(value, axis, pairs)  34.3 us
    pallas_call x6, Pallas kernels, cross_part(): pl.pallas_call(lambda *refs: cross_kernel(mine, keep, *refs), out_shape=j...  21.8 us
    ppermute x14, starting transfers between devices, passed_along(): return lax.ppermute(value, axis, pairs)  13.5 us
    pallas_call x4, Pallas kernels, forward(): pl.pallas_call(lambda *refs: forward_kernel(half, padded, rotated, *refs)...  12.4 us
    pallas_call x3, Pallas kernels, inverse(): pl.pallas_call(lambda *refs: inverse_kernel(padded, *refs), out_shape=jax...  9.45 us
    convert_element_type x2, other arithmetic, other_channels(): return passed_along(theirs.astype(BF16), 'fft', 1)  2.75 us
    unnamed x26, local copies, waits for them, and re-layouts  2.13 us
  transfers between devices with their start and end apart: 14, of which 6 were waited for; matrix products, arithmetic and copies ran while one was open for 3% of the time, Pallas kernels for 37%

profile of v1, /device:TPU:0, one launch (start us, length us, event | category | flops | bytes accessed | tf_op | source)
XLA Modules:
  0.0 100.2 jit_solution(5464025537931601932)
XLA Ops:
  0.0 1.4 %fusion = bf16[2,32,4096]{2,1,0:T(8,128)(2,1)S(1)} fusion(s32[1,4,32,4096]{3,2,1,0:T(8,128)} %refs_2_.9, s32[]{:T(128)S(6)} %select_n.30), kind=kLoop, calls=%fused_computation.2 | loop fusion | flops 262144 | bytes 1572868 | tf_op jit(solution)/shard_map/convert_element_type | solution.py:347
  1.4 0.0 copy-start.1
  1.5 0.6 collective-permute-start.2
  2.0 1.3 %fusion.1 = bf16[2,32,4096]{2,1,0:T(8,128)(2,1)S(1)} fusion(s32[1,4,32,4096]{3,2,1,0:T(8,128)} %refs_2_.10, s32[]{:T(128)S(6)} %select_n.30), kind=kLoop, calls=%fused_computation.3 | loop fusion | flops 262144 | bytes 1572868 | tf_op jit(solution)/shard_map/convert_element_type | solution.py:347
  3.4 0.2 collective-permute-start.3
  4.2 0.0 collective-permute-done.2.refs_3_
  4.2 0.0 copy-done.8
  4.2 0.0 copy-done.7
  4.2 0.0 copy-done.6
  4.2 0.0 copy-done
  4.2 2.5 %forward_receptor.2.refs_7_.refs_2_ = bf16[33,64,128]{2,1,0:T(8,128)(2,1)S(1)} custom-call(s32[1]{0:T(128)} %bitcast.refs_0_, s32[1]{0:T(128)S(6)} %copy.12.refs_1_, s32[1,4,32,4096]{3,2,1,0:T(8,128)S(1)} %copy-done, bf16[2,32,4096]{2,1,0:T(8,128)(2,1)S(1)} %collective-permute-done.2.refs_3_, bf16[2,80,64]{2,1,0:T(8,128)(2,1)S(1)} %copy-done.8, ...), custom_call_target="tpu_custom_call" | custom-call | flops 207618048 | bytes 2621440 | tf_op jit(solution)/shard_map/forward_receptor/pallas_call | solution.py:159
  6.8 0.0 copy-start.2
  6.8 3.0 %collective-permute-start.6 = (bf16[33,64,128]{2,1,0:T(8,128)(2,1)S(1)}, bf16[33,64,128]{2,1,0:T(8,128)(2,1)}, u32[]{:S(2)}, u32[]{:S(2)}) collective-permute-start(bf16[33,64,128]{2,1,0:T(8,128)(2,1)S(1)} %forward_receptor.2.refs_7_.refs_2_), channel_id=1, source_target_pairs={{0,4},{4,8},{8,12},{12,0},{1,5},{5,9},{9,13},{13,1},{2,6},{6,10},{... | collective-permute-start | bytes 1622024 | tf_op jit(solution)/shard_map/ppermute | solution.py:22
  9.8 0.0 collective-permute-done.3.refs_3_
  9.8 0.0 copy-done.1
  9.8 3.7 %forward_pose.2.refs_7_.refs_4_ = bf16[33,64,128]{2,1,0:T(8,128)(2,1)S(1)} custom-call(s32[1]{0:T(128)} %bitcast.refs_0_, s32[1]{0:T(128)S(6)} %copy.12.refs_1_, s32[1,4,32,4096]{3,2,1,0:T(8,128)S(1)} %copy-done.1, bf16[2,32,4096]{2,1,0:T(8,128)(2,1)S(1)} %collective-permute-done.3.refs_3_, bf16[2,80,64]{2,1,0:T(8,128)(2,1)S(1)} %copy-done.8, ...), custom_call_target="tpu_custom_call" | custom-call | flops 207618048 | bytes 2621440 | tf_op jit(solution)/shard_map/forward_pose/pallas_call | solution.py:159
  13.4 2.5 %forward_receptor.3.refs_7_.refs_3_ = bf16[33,64,128]{2,1,0:T(8,128)(2,1)S(1)} custom-call(s32[1]{0:T(128)} %bitcast.refs_0_, s32[1]{0:T(128)S(6)} %copy.12.refs_1_, s32[1,4,32,4096]{3,2,1,0:T(8,128)S(1)} %copy-done, bf16[2,32,4096]{2,1,0:T(8,128)(2,1)S(1)} %collective-permute-done.2.refs_3_, bf16[2,80,64]{2,1,0:T(8,128)(2,1)S(1)} %copy-done.8, ...), custom_call_target="tpu_custom_call" | custom-call | flops 207618048 | bytes 2621440 | tf_op jit(solution)/shard_map/forward_receptor/pallas_call | solution.py:159
  16.0 0.0 copy-start.4
  16.0 0.0 copy-start.12
  16.0 1.6 %collective-permute-start.7 = (bf16[33,64,128]{2,1,0:T(8,128)(2,1)S(1)}, bf16[33,64,128]{2,1,0:T(8,128)(2,1)}, u32[]{:S(2)}, u32[]{:S(2)}) collective-permute-start(bf16[33,64,128]{2,1,0:T(8,128)(2,1)S(1)} %forward_receptor.3.refs_7_.refs_3_), channel_id=1, source_target_pairs={{0,4},{4,8},{8,12},{12,0},{1,5},{5,9},{9,13},{13,1},{2,6},{6,10},{... | collective-permute-start | bytes 1622024 | tf_op jit(solution)/shard_map/ppermute | solution.py:22
  17.6 3.7 %forward_pose.3.refs_1_.refs_5_ = bf16[33,64,128]{2,1,0:T(8,128)(2,1)S(1)} custom-call(s32[1]{0:T(128)} %bitcast.refs_0_, s32[1]{0:T(128)S(6)} %copy.12.refs_1_, s32[1,4,32,4096]{3,2,1,0:T(8,128)S(1)} %copy-done.1, bf16[2,32,4096]{2,1,0:T(8,128)(2,1)S(1)} %collective-permute-done.3.refs_3_, bf16[2,80,64]{2,1,0:T(8,128)(2,1)S(1)} %copy-done.8, ...), custom_call_target="tpu_custom_call" | custom-call | flops 207618048 | bytes 2621440 | tf_op jit(solution)/shard_map/forward_pose/pallas_call | solution.py:159
  21.3 0.1 collective-permute-start.5
  21.4 2.0 %collective-permute-start.4 = (bf16[33,64,128]{2,1,0:T(8,128)(2,1)S(1)}, bf16[33,64,128]{2,1,0:T(8,128)(2,1)S(1)}, u32[]{:S(2)}, u32[]{:S(2)}) collective-permute-start(bf16[33,64,128]{2,1,0:T(8,128)(2,1)S(1)} %forward_pose.2.refs_7_.refs_4_), channel_id=1, source_target_pairs={{0,2},{2,0},{1,3},{3,1},{4,6},{6,4},{5,7},{7,5},{8,10},{10,8},{9,1... | collective-permute-start | bytes 1622024 | tf_op jit(solution)/shard_map/ppermute | solution.py:22
  23.4 1.6 %collective-permute-done.6.refs_0_.refs_2_ = bf16[33,64,128]{2,1,0:T(8,128)(2,1)} collective-permute-done((bf16[33,64,128]{2,1,0:T(8,128)(2,1)S(1)}, bf16[33,64,128]{2,1,0:T(8,128)(2,1)}, u32[]{:S(2)}, u32[]{:S(2)}) %collective-permute-start.6) | collective-permute-done | bytes 540704 | tf_op jit(solution)/shard_map/ppermute | solution.py:22
  25.0 11.1 %collective-permute-done.7.refs_0_.refs_3_ = bf16[33,64,128]{2,1,0:T(8,128)(2,1)} collective-permute-done((bf16[33,64,128]{2,1,0:T(8,128)(2,1)S(1)}, bf16[33,64,128]{2,1,0:T(8,128)(2,1)}, u32[]{:S(2)}, u32[]{:S(2)}) %collective-permute-start.7) | collective-permute-done | bytes 540704 | tf_op jit(solution)/shard_map/ppermute | solution.py:22
  36.1 0.4 collective-permute-done.5.refs_7_
  36.5 10.2 %collective-permute-done.4.refs_6_ = bf16[33,64,128]{2,1,0:T(8,128)(2,1)S(1)} collective-permute-done((bf16[33,64,128]{2,1,0:T(8,128)(2,1)S(1)}, bf16[33,64,128]{2,1,0:T(8,128)(2,1)S(1)}, u32[]{:S(2)}, u32[]{:S(2)}) %collective-permute-start.4) | collective-permute-done | bytes 540704 | tf_op jit(solution)/shard_map/ppermute | solution.py:22
  46.7 0.0 copy-done.12
  46.7 4.4 %cross_send.3.refs_8_ = bf16[33,64,128]{2,1,0:T(8,128)(2,1)} custom-call(s32[1]{0:T(128)} %bitcast.refs_0_, f32[4]{0:T(128)S(1)} %copy-done.12, bf16[33,64,128]{2,1,0:T(8,128)(2,1)} %collective-permute-done.6.refs_0_.refs_2_, bf16[33,64,128]{2,1,0:T(8,128)(2,1)} %collective-permute-done.7.refs_0_.refs_3_, ...), custom_call_target="tpu_custom_call" | custom-call | flops 5406720 | bytes 3784704 | tf_op jit(solution)/shard_map/cross_send/pallas_call | solution.py:237
  51.1 0.0 collective-permute-start.9
  51.1 3.6 %cross_keep.3.refs_8_.refs_0_ = f32[33,64,128]{2,1,0:T(8,128)S(1)} custom-call(s32[1]{0:T(128)} %bitcast.refs_0_, f32[4]{0:T(128)S(1)} %copy-done.12, bf16[33,64,128]{2,1,0:T(8,128)(2,1)} %collective-permute-done.6.refs_0_.refs_2_, bf16[33,64,128]{2,1,0:T(8,128)(2,1)} %collective-permute-done.7.refs_0_.refs_3_, ...), custom_call_target="tpu_custom_call" | custom-call | flops 5406720 | bytes 3784704 | tf_op jit(solution)/shard_map/cross_keep/pallas_call | solution.py:237
  54.7 0.0 copy-done.2
  54.8 0.0 copy-done.4
  54.8 3.6 %cross_send.4.refs_8_ = bf16[33,64,128]{2,1,0:T(8,128)(2,1)} custom-call(s32[1]{0:T(128)} %bitcast.refs_0_, f32[4]{0:T(128)S(1)} %copy-done.12, bf16[33,64,128]{2,1,0:T(8,128)(2,1)S(1)} %forward_receptor.2.refs_7_.refs_2_, bf16[33,64,128]{2,1,0:T(8,128)(2,1)S(1)} %forward_receptor.3.refs_7_.refs_3_, bf16[33,64,128]{2,1,0:T(8,128)(2,1)S(1)} %forward_pose.2.refs_7_.refs_4_, ...), custom_call_target="tpu_custom_call" | custom-call | flops 5406720 | bytes 3784704 | tf_op jit(solution)/shard_map/cross_send/pallas_call | solution.py:237
  58.4 0.5 collective-permute-start.8
  58.9 0.5 collective-permute-start.11
  59.4 0.3 collective-permute-start.10
  59.7 2.6 %collective-permute-start = (s32[1]{0:T(128)}, s32[1]{0:T(128)}, u32[]{:S(2)}, u32[]{:S(2)}) collective-permute-start(s32[1]{0:T(128)} %param.14), channel_id=1, source_target_pairs={{0,4},{4,8},{8,12},{12,0},{1,5},{5,9},{9,13},{13,1},{2,6},{6,10},{... | collective-permute-start | bytes 20 | tf_op jit(solution)/shard_map/ppermute | solution.py:22
  63.0 0.0 copy-start.3
  63.0 1.0 %copy-done.3 = bf16[33,64,128]{2,1,0:T(8,128)(2,1)S(1)} copy-done((bf16[33,64,128]{2,1,0:T(8,128)(2,1)S(1)}, bf16[33,64,128]{2,1,0:T(8,128)(2,1)}, u32[]{:S(2)}) %copy-start.3) | copy-done | bytes 540696
  64.0 1.0 %copy-done.5 = bf16[33,64,128]{2,1,0:T(8,128)(2,1)S(1)} copy-done((bf16[33,64,128]{2,1,0:T(8,128)(2,1)S(1)}, bf16[33,64,128]{2,1,0:T(8,128)(2,1)}, u32[]{:S(2)}) %copy-start.5) | copy-done | bytes 540696
  65.1 2.9 %cross_keep.4.refs_5_.refs_0_ = f32[33,64,128]{2,1,0:T(8,128)S(1)} custom-call(s32[1]{0:T(128)} %bitcast.refs_0_, f32[4]{0:T(128)S(1)} %copy-done.12, bf16[33,64,128]{2,1,0:T(8,128)(2,1)S(1)} %copy-done.3, bf16[33,64,128]{2,1,0:T(8,128)(2,1)S(1)} %copy-done.5, bf16[33,64,128]{2,1,0:T(8,128)(2,1)S(1)} %forward_pose.2.refs_7_.refs_4_, ...), custom_call_target="tpu_custom_call" | custom-call | flops 5406720 | bytes 3784704 | tf_op jit(solution)/shard_map/cross_keep/pallas_call | solution.py:237
  68.0 0.0 collective-permute-done.9.refs_1_
  68.0 1.5 %collective-permute-start.1 = (s32[1]{0:T(128)}, s32[1]{0:T(128)}, u32[]{:S(2)}, u32[]{:S(2)}) collective-permute-start(s32[1]{0:T(128)} %param.14), channel_id=1, source_target_pairs={{0,8},{4,12},{8,0},{12,4},{1,9},{5,13},{9,1},{13,5},{2,10},{6,14},... | collective-permute-start | bytes 20 | tf_op jit(solution)/shard_map/ppermute | solution.py:22
  69.6 0.0 copy-done.9
  69.6 3.5 %inverse_pair.3.refs_5_ = f32[1,64]{1,0:T(1,128)S(1)} custom-call(f32[33,64,128]{2,1,0:T(8,128)S(1)} %cross_keep.3.refs_8_.refs_0_, bf16[33,64,128]{2,1,0:T(8,128)(2,1)} %collective-permute-done.9.refs_1_, bf16[64,80]{1,0:T(8,128)(2,1)S(1)} %copy-done.11, bf16[128,64]{1,0:T(8,128)(2,1)S(1)} %copy-done.10, bf16[256,128]{1,0:T(8,128)(2,1)S(1)} %copy-done.9, ...), custom_call_target="tpu_custom_call" | custom-call | flops 207618048 | bytes 4325376 | tf_op jit(solution)/shard_map/inverse_pair/pallas_call | solution.py:297
  73.1 0.0 collective-permute-done.8.refs_1_
  73.1 3.5 %inverse_pair.4.refs_8_ = f32[1,64]{1,0:T(1,128)S(1)} custom-call(f32[33,64,128]{2,1,0:T(8,128)S(1)} %cross_keep.4.refs_5_.refs_0_, bf16[33,64,128]{2,1,0:T(8,128)(2,1)} %collective-permute-done.8.refs_1_, bf16[64,80]{1,0:T(8,128)(2,1)S(1)} %copy-done.11, bf16[128,64]{1,0:T(8,128)(2,1)S(1)} %copy-done.10, bf16[256,128]{1,0:T(8,128)(2,1)S(1)} %copy-done.9, ...), custom_call_target="tpu_custom_call" | custom-call | flops 207618048 | bytes 4325376 | tf_op jit(solution)/shard_map/inverse_pair/pallas_call | solution.py:297
  76.6 0.0 collective-permute-done.11.refs_3_
  76.6 10.2 %collective-permute-done.10.refs_2_ = bf16[33,64,128]{2,1,0:T(8,128)(2,1)} collective-permute-done((bf16[33,64,128]{2,1,0:T(8,128)(2,1)}, bf16[33,64,128]{2,1,0:T(8,128)(2,1)}, u32[]{:S(2)}, u32[]{:S(2)}) %collective-permute-start.10) | collective-permute-done | bytes 540704 | tf_op jit(solution)/shard_map/ppermute | solution.py:22
  86.8 3.6 %cross_send.5.refs_8_ = bf16[33,64,128]{2,1,0:T(8,128)(2,1)S(1)} custom-call(s32[1]{0:T(128)} %bitcast.refs_0_, f32[4]{0:T(128)S(1)} %copy-done.12, bf16[33,64,128]{2,1,0:T(8,128)(2,1)} %collective-permute-done.10.refs_2_, bf16[33,64,128]{2,1,0:T(8,128)(2,1)} %collective-permute-done.11.refs_3_, bf16[33,64,128]{2,1,0:T(8,128)(2,1)S(1)} %forward_pose.2.refs_7_.refs_4_, ...), custom_call_target="tpu_custom_call" | custom-call | flops 5406720 | bytes 3784704 | tf_op jit(solution)/shard_map/cross_send/pallas_call | solution.py:237
  90.5 0.1 collective-permute-start.12
  90.6 0.0 collective-permute-done
  90.6 0.0 collective-permute-done.1
  90.6 1.3 %pad_add_fusion = s32[3]{0:T(128)S(1)} fusion(s32[1]{0:T(128)} %collective-permute-done.1, s32[1]{0:T(128)} %collective-permute-done, s32[1]{0:T(128)S(6)} %copy.13), kind=kLoop, calls=%fused_computation.9 | loop fusion | flops 6 | bytes 24 | tf_op jit(solution)/shard_map/concatenate | solution.py:406
  91.9 0.1 broadcast_compare_fusion
  92.0 3.6 %cross_keep.5.refs_0_.refs_5_ = f32[33,64,128]{2,1,0:T(8,128)S(1)} custom-call(s32[1]{0:T(128)} %bitcast.refs_0_, f32[4]{0:T(128)S(1)} %copy-done.12, bf16[33,64,128]{2,1,0:T(8,128)(2,1)} %collective-permute-done.10.refs_2_, bf16[33,64,128]{2,1,0:T(8,128)(2,1)} %collective-permute-done.11.refs_3_, bf16[33,64,128]{2,1,0:T(8,128)(2,1)S(1)} %forward_pose.2.refs_7_.refs_4_, ...), custom_call_target="tpu_custom_call" | custom-call | flops 5406720 | bytes 3784704 | tf_op jit(solution)/shard_map/cross_keep/pallas_call | solution.py:237
  95.6 0.0 collective-permute-done.12.refs_1_
  95.6 2.5 %inverse_pair.5 = f32[1,64]{1,0:T(1,128)S(1)} custom-call(f32[33,64,128]{2,1,0:T(8,128)S(1)} %cross_keep.5.refs_0_.refs_5_, bf16[33,64,128]{2,1,0:T(8,128)(2,1)S(1)} %collective-permute-done.12.refs_1_, bf16[64,80]{1,0:T(8,128)(2,1)S(1)} %copy-done.11, bf16[128,64]{1,0:T(8,128)(2,1)S(1)} %copy-done.10, bf16[256,128]{1,0:T(8,128)(2,1)S(1)} %copy-done.9, ...), custom_call_target="tpu_custom_call" | custom-call | flops 207618048 | bytes 4325376 | tf_op jit(solution)/shard_map/inverse_pair/pallas_call | solution.py:297
  98.1 0.5 collective-permute-start.13
  98.7 0.1 constant_dynamic-slice_fusion.1
  98.7 0.7 collective-permute-done.13
  99.5 0.1 constant_dynamic-slice_fusion
  99.5 0.7 select_select_fusion
  (15 shorter events, 0.0 us)
Async XLA Ops:
  0.0 4.2 %copy-start.8 = (bf16[2,80,64]{2,1,0:T(8,128)(2,1)S(1)}, bf16[2,80,64]{2,1,0:T(8,128)(2,1)}, u32[]{:S(2)}) copy-start(bf16[2,80,64]{2,1,0:T(8,128)(2,1)} %constant.32.clone.refs_4_) | copy-start | bytes 61444
  0.0 4.2 %copy-start.7 = (bf16[2,128,64]{2,1,0:T(8,128)(2,1)S(1)}, bf16[2,128,64]{2,1,0:T(8,128)(2,1)}, u32[]{:S(2)}) copy-start(bf16[2,128,64]{2,1,0:T(8,128)(2,1)} %constant.33.clone.refs_5_) | copy-start | bytes 98308
  0.0 4.2 %copy-start.6 = (bf16[2,256,128]{2,1,0:T(8,128)(2,1)S(1)}, bf16[2,256,128]{2,1,0:T(8,128)(2,1)}, u32[]{:S(2)}) copy-start(bf16[2,256,128]{2,1,0:T(8,128)(2,1)} %constant.34.clone.refs_6_) | copy-start | bytes 393220
  0.0 4.2 %copy-start = (s32[1,4,32,4096]{3,2,1,0:T(8,128)S(1)}, s32[1,4,32,4096]{3,2,1,0:T(8,128)}, u32[]{:S(2)}) copy-start(s32[1,4,32,4096]{3,2,1,0:T(8,128)} %refs_2_.9) | copy-start | bytes 6291460
  1.4 8.3 %copy-start.1 = (s32[1,4,32,4096]{3,2,1,0:T(8,128)S(1)}, s32[1,4,32,4096]{3,2,1,0:T(8,128)}, u32[]{:S(2)}) copy-start(s32[1,4,32,4096]{3,2,1,0:T(8,128)} %refs_2_.10) | copy-start | bytes 6291460
  1.5 2.7 %collective-permute-start.2 = (bf16[2,32,4096]{2,1,0:T(8,128)(2,1)S(1)}, bf16[2,32,4096]{2,1,0:T(8,128)(2,1)S(1)}, u32[]{:S(2)}, u32[]{:S(2)}) collective-permute-start(bf16[2,32,4096]{2,1,0:T(8,128)(2,1)S(1)} %fusion), channel_id=1, source_target_pairs={{0,1},{1,0},{2,3},{3,2},{4,5},{5,4},{6,7},{7,6},{8,9},{9,8},{10,11... | collective-permute-start | bytes 1572872 | tf_op jit(solution)/shard_map/ppermute | solution.py:22
  3.4 6.4 %collective-permute-start.3 = (bf16[2,32,4096]{2,1,0:T(8,128)(2,1)S(1)}, bf16[2,32,4096]{2,1,0:T(8,128)(2,1)S(1)}, u32[]{:S(2)}, u32[]{:S(2)}) collective-permute-start(bf16[2,32,4096]{2,1,0:T(8,128)(2,1)S(1)} %fusion.1), channel_id=1, source_target_pairs={{0,1},{1,0},{2,3},{3,2},{4,5},{5,4},{6,7},{7,6},{8,9},{9,8},{10,11... | collective-permute-start | bytes 1572872 | tf_op jit(solution)/shard_map/ppermute | solution.py:22
  6.8 48.0 %copy-start.2 = (bf16[33,64,128]{2,1,0:T(8,128)(2,1)}, bf16[33,64,128]{2,1,0:T(8,128)(2,1)S(1)}, u32[]{:S(2)}) copy-start(bf16[33,64,128]{2,1,0:T(8,128)(2,1)S(1)} %forward_receptor.2.refs_7_.refs_2_) | copy-start | bytes 1622020
  6.8 18.2 %collective-permute-start.6 = (bf16[33,64,128]{2,1,0:T(8,128)(2,1)S(1)}, bf16[33,64,128]{2,1,0:T(8,128)(2,1)}, u32[]{:S(2)}, u32[]{:S(2)}) collective-permute-start(bf16[33,64,128]{2,1,0:T(8,128)(2,1)S(1)} %forward_receptor.2.refs_7_.refs_2_), channel_id=1, source_target_pairs={{0,4},{4,8},{8,12},{12,0},{1,5},{5,9},{9,13},{13,1},{2,6},{6,10},{... | collective-permute-start | bytes 1622024 | tf_op jit(solution)/shard_map/ppermute | solution.py:22
  16.0 38.8 %copy-start.4 = (bf16[33,64,128]{2,1,0:T(8,128)(2,1)}, bf16[33,64,128]{2,1,0:T(8,128)(2,1)S(1)}, u32[]{:S(2)}) copy-start(bf16[33,64,128]{2,1,0:T(8,128)(2,1)S(1)} %forward_receptor.3.refs_7_.refs_3_) | copy-start | bytes 1622020
  16.0 30.8 %copy-start.12 = (f32[4]{0:T(128)S(1)}, f32[4]{0:T(128)}, u32[]{:S(2)}) copy-start(f32[4]{0:T(128)} %refs_1_.15) | copy-start | bytes 52
  16.0 20.1 %collective-permute-start.7 = (bf16[33,64,128]{2,1,0:T(8,128)(2,1)S(1)}, bf16[33,64,128]{2,1,0:T(8,128)(2,1)}, u32[]{:S(2)}, u32[]{:S(2)}) collective-permute-start(bf16[33,64,128]{2,1,0:T(8,128)(2,1)S(1)} %forward_receptor.3.refs_7_.refs_3_), channel_id=1, source_target_pairs={{0,4},{4,8},{8,12},{12,0},{1,5},{5,9},{9,13},{13,1},{2,6},{6,10},{... | collective-permute-start | bytes 1622024 | tf_op jit(solution)/shard_map/ppermute | solution.py:22
  21.3 15.2 %collective-permute-start.5 = (bf16[33,64,128]{2,1,0:T(8,128)(2,1)S(1)}, bf16[33,64,128]{2,1,0:T(8,128)(2,1)S(1)}, u32[]{:S(2)}, u32[]{:S(2)}) collective-permute-start(bf16[33,64,128]{2,1,0:T(8,128)(2,1)S(1)} %forward_pose.3.refs_1_.refs_5_), channel_id=1, source_target_pairs={{0,2},{2,0},{1,3},{3,1},{4,6},{6,4},{5,7},{7,5},{8,10},{10,8},{9,1... | collective-permute-start | bytes 1622024 | tf_op jit(solution)/shard_map/ppermute | solution.py:22
  21.4 25.4 %collective-permute-start.4 = (bf16[33,64,128]{2,1,0:T(8,128)(2,1)S(1)}, bf16[33,64,128]{2,1,0:T(8,128)(2,1)S(1)}, u32[]{:S(2)}, u32[]{:S(2)}) collective-permute-start(bf16[33,64,128]{2,1,0:T(8,128)(2,1)S(1)} %forward_pose.2.refs_7_.refs_4_), channel_id=1, source_target_pairs={{0,2},{2,0},{1,3},{3,1},{4,6},{6,4},{5,7},{7,5},{8,10},{10,8},{9,1... | collective-permute-start | bytes 1622024 | tf_op jit(solution)/shard_map/ppermute | solution.py:22
  51.1 16.9 %collective-permute-start.9 = (bf16[33,64,128]{2,1,0:T(8,128)(2,1)}, bf16[33,64,128]{2,1,0:T(8,128)(2,1)}, u32[]{:S(2)}, u32[]{:S(2)}) collective-permute-start(bf16[33,64,128]{2,1,0:T(8,128)(2,1)} %cross_send.3.refs_8_), channel_id=1, source_target_pairs={{0,1},{1,0},{2,3},{3,2},{4,5},{5,4},{6,7},{7,6},{8,9},{9,8},{10,11... | collective-permute-start | bytes 1622024 | tf_op jit(solution)/shard_map/ppermute | solution.py:22
  58.4 14.7 %collective-permute-start.8 = (bf16[33,64,128]{2,1,0:T(8,128)(2,1)}, bf16[33,64,128]{2,1,0:T(8,128)(2,1)}, u32[]{:S(2)}, u32[]{:S(2)}) collective-permute-start(bf16[33,64,128]{2,1,0:T(8,128)(2,1)} %cross_send.4.refs_8_), channel_id=1, source_target_pairs={{0,1},{1,0},{2,3},{3,2},{4,5},{5,4},{6,7},{7,6},{8,9},{9,8},{10,11... | collective-permute-start | bytes 1622024 | tf_op jit(solution)/shard_map/ppermute | solution.py:22
  58.9 17.7 %collective-permute-start.11 = (bf16[33,64,128]{2,1,0:T(8,128)(2,1)}, bf16[33,64,128]{2,1,0:T(8,128)(2,1)}, u32[]{:S(2)}, u32[]{:S(2)}) collective-permute-start(bf16[33,64,128]{2,1,0:T(8,128)(2,1)} %collective-permute-done.7.refs_0_.refs_3_), channel_id=1, source_target_pairs={{0,4},{4,8},{8,12},{12,0},{1,5},{5,9},{9,13},{13,1},{2,6},{6,10},{... | collective-permute-start | bytes 1622024 | tf_op jit(solution)/shard_map/ppermute | solution.py:22
  59.4 27.5 %collective-permute-start.10 = (bf16[33,64,128]{2,1,0:T(8,128)(2,1)}, bf16[33,64,128]{2,1,0:T(8,128)(2,1)}, u32[]{:S(2)}, u32[]{:S(2)}) collective-permute-start(bf16[33,64,128]{2,1,0:T(8,128)(2,1)} %collective-permute-done.6.refs_0_.refs_2_), channel_id=1, source_target_pairs={{0,4},{4,8},{8,12},{12,0},{1,5},{5,9},{9,13},{13,1},{2,6},{6,10},{... | collective-permute-start | bytes 1622024 | tf_op jit(solution)/shard_map/ppermute | solution.py:22
  59.7 30.9 %collective-permute-start = (s32[1]{0:T(128)}, s32[1]{0:T(128)}, u32[]{:S(2)}, u32[]{:S(2)}) collective-permute-start(s32[1]{0:T(128)} %param.14), channel_id=1, source_target_pairs={{0,4},{4,8},{8,12},{12,0},{1,5},{5,9},{9,13},{13,1},{2,6},{6,10},{... | collective-permute-start | bytes 20 | tf_op jit(solution)/shard_map/ppermute | solution.py:22
  63.0 1.0 %copy-start.3 = (bf16[33,64,128]{2,1,0:T(8,128)(2,1)S(1)}, bf16[33,64,128]{2,1,0:T(8,128)(2,1)}, u32[]{:S(2)}) copy-start(bf16[33,64,128]{2,1,0:T(8,128)(2,1)} %copy-done.2) | copy-start | bytes 1622020
  64.0 1.0 %copy-start.5 = (bf16[33,64,128]{2,1,0:T(8,128)(2,1)S(1)}, bf16[33,64,128]{2,1,0:T(8,128)(2,1)}, u32[]{:S(2)}) copy-start(bf16[33,64,128]{2,1,0:T(8,128)(2,1)} %copy-done.4) | copy-start | bytes 1622020
  65.1 4.5 %copy-start.9 = (bf16[256,128]{1,0:T(8,128)(2,1)S(1)}, bf16[256,128]{1,0:T(8,128)(2,1)}, u32[]{:S(2)}) copy-start(bf16[256,128]{1,0:T(8,128)(2,1)} %constant.37.clone.refs_4_) | copy-start | bytes 196612
  65.1 4.5 %copy-start.10 = (bf16[128,64]{1,0:T(8,128)(2,1)S(1)}, bf16[128,64]{1,0:T(8,128)(2,1)}, u32[]{:S(2)}) copy-start(bf16[128,64]{1,0:T(8,128)(2,1)} %constant.36.clone.refs_3_) | copy-start | bytes 49156
  65.1 4.5 %copy-start.11 = (bf16[64,80]{1,0:T(8,128)(2,1)S(1)}, bf16[64,80]{1,0:T(8,128)(2,1)}, u32[]{:S(2)}) copy-start(bf16[64,80]{1,0:T(8,128)(2,1)} %constant.35.clone.refs_2_) | copy-start | bytes 30724
  68.0 22.5 %collective-permute-start.1 = (s32[1]{0:T(128)}, s32[1]{0:T(128)}, u32[]{:S(2)}, u32[]{:S(2)}) collective-permute-start(s32[1]{0:T(128)} %param.14), channel_id=1, source_target_pairs={{0,8},{4,12},{8,0},{12,4},{1,9},{5,13},{9,1},{13,5},{2,10},{6,14},... | collective-permute-start | bytes 20 | tf_op jit(solution)/shard_map/ppermute | solution.py:22
  90.5 5.2 %collective-permute-start.12 = (bf16[33,64,128]{2,1,0:T(8,128)(2,1)S(1)}, bf16[33,64,128]{2,1,0:T(8,128)(2,1)S(1)}, u32[]{:S(2)}, u32[]{:S(2)}) collective-permute-start(bf16[33,64,128]{2,1,0:T(8,128)(2,1)S(1)} %cross_send.5.refs_8_), channel_id=1, source_target_pairs={{0,1},{1,0},{2,3},{3,2},{4,5},{5,4},{6,7},{7,6},{8,9},{9,8},{10,11... | collective-permute-start | bytes 1622024 | tf_op jit(solution)/shard_map/ppermute | solution.py:22
  98.1 1.4 %collective-permute-start.13 = (f32[3,64]{1,0:T(4,128)S(1)}, f32[3,64]{1,0:T(4,128)S(1)}, u32[]{:S(2)}, u32[]{:S(2)}) collective-permute-start(f32[3,64]{1,0:T(4,128)S(1)} %pad_maximum_fusion), channel_id=1, source_target_pairs={{0,1},{1,0},{2,3},{3,2},{4,5},{5,4},{6,7},{7,6},{8,9},{9,8},{10,11... | collective-permute-start | bytes 2312 | tf_op jit(solution)/shard_map/ppermute | solution.py:22

commit v2 on v1

--- a/solution.py
+++ b/solution.py
@@ -170,20 +170,20 @@
     )(core, turns, occupancy, received, *tables, *after)
 
 
-def partial_cross(scales, receptors, ligands, where, cells):
+def partial_cross(scales, receptors, ligands, exchange, where, cells):
     same = None
     swapped = None
     for scale, receptor, ligand in zip(scales, receptors, ligands):
         left = receptor[where].astype(F32) * scale
-        right = ligand(where).astype(F32)
-        turned = pltpu.roll(right, cells, right.ndim - 1)
+        right = ligand(where)
+        turned = jnp.dot(right, exchange, preferred_element_type=F32)
+        right = right.astype(F32)
         same = left * right if same is None else same + left * right
         swapped = left * turned if swapped is None else swapped + left * turned
     axis = same.ndim - 1
     low = lax.broadcasted_iota(jnp.int32, same.shape, axis) < cells
-    real = same + pltpu.roll(same, cells, axis)
-    imag = swapped - pltpu.roll(swapped, cells, axis)
-    return jnp.where(low, real, imag)
+    across = pltpu.roll(jnp.where(low, -swapped, same), cells, axis)
+    return jnp.where(low, same, swapped) + across
 
 
 def chosen(pick_second, first, second):
@@ -193,14 +193,17 @@
 def cross_kernel(mine, keep, core, weights, *refs):
     receptors, firsts, seconds = refs[:mine], refs[mine : 2 * mine], refs[2 * mine : 3 * mine]
     out = refs[-1]
-    group, cells, _ = out.shape
+    group, cells, lanes = out.shape
     volume = 1.0 / float(cells) ** 3
     scales = [weights[core[0] * mine + c] * volume for c in range(mine)]
     second = core[0] == int(keep)
     ligands = [chosen(second, *pair) for pair in zip(firsts, seconds)]
 
+    row = lax.broadcasted_iota(jnp.int32, (lanes, lanes), 0)
+    column = lax.broadcasted_iota(jnp.int32, (lanes, lanes), 1)
+    exchange = jnp.where((row + cells) % lanes == column, 1.0, 0.0).astype(BF16)
     for k in range(group):
-        out[k] = partial_cross(scales, receptors, ligands, k, cells).astype(out.dtype)
+        out[k] = partial_cross(scales, receptors, ligands, exchange, k, cells).astype(out.dtype)
 
 
 def vmem():

time: 101 us -> 96.9 us (0.959)
  Pallas kernels: 43.7 us -> 38.8 us
  waiting for transfers between devices: 34.3 us -> 35.4 us
    pallas_call x6, Pallas kernels: 21.8 us -> 17 us  [cross_part(): pl.pallas_call(lambda *refs: cross_kernel(mine, keep, *refs), out_shape=j...]
    ppermute x14, waiting for transfers between devices: 34.3 us -> 35.4 us  [passed_along(): return lax.ppermute(value, axis, pairs)]
  transfers between devices with their start and end apart: 14 -> 14, of which waited for: 6 -> 7; matrix products, arithmetic and copies ran while one was open for 3% -> 3% of each run, Pallas kernels for 37% -> 34%
where the time goes in v2:
time: 96.9 us; the launch traced here: 96.4 us
  Pallas kernels  38.8 us (40%)
  waiting for transfers between devices  35.4 us (37%)
  starting transfers between devices  13.5 us (14%)
  other arithmetic  4.81 us (5%)
  local copies, waits for them, and re-layouts  2.28 us (2%)
  between operations  1.61 us (2%)
    ppermute x14, waiting for transfers between devices, passed_along(): return lax.ppermute(value, axis, pairs)  35.4 us
    pallas_call x6, Pallas kernels, cross_part(): pl.pallas_call(lambda *refs: cross_kernel(mine, keep, *refs), out_shape=j...  17 us
    ppermute x14, starting transfers between devices, passed_along(): return lax.ppermute(value, axis, pairs)  13.5 us
    pallas_call x4, Pallas kernels, forward(): pl.pallas_call(lambda *refs: forward_kernel(half, padded, rotated, *refs)...  12.4 us
    pallas_call x3, Pallas kernels, inverse(): pl.pallas_call(lambda *refs: inverse_kernel(padded, *refs), out_shape=jax...  9.45 us
    convert_element_type x2, other arithmetic, other_channels(): return passed_along(theirs.astype(BF16), 'fft', 1)  2.75 us
    unnamed x26, local copies, waits for them, and re-layouts  2.13 us
  transfers between devices with their start and end apart: 14, of which 7 were waited for; matrix products, arithmetic and copies ran while one was open for 3% of the time, Pallas kernels for 34%

profile of v2, /device:TPU:0, one launch (start us, length us, event | category | flops | bytes accessed | tf_op | source)
XLA Modules:
  0.0 96.4 jit_solution(17438448037116856804)
XLA Ops:
  0.0 1.4 %fusion = bf16[2,32,4096]{2,1,0:T(8,128)(2,1)S(1)} fusion(s32[1,4,32,4096]{3,2,1,0:T(8,128)} %refs_2_.9, s32[]{:T(128)S(6)} %select_n.30), kind=kLoop, calls=%fused_computation.2 | loop fusion | flops 262144 | bytes 1572868 | tf_op jit(solution)/shard_map/convert_element_type | solution.py:350
  1.4 0.0 copy-start.1
  1.5 0.6 collective-permute-start.2
  2.0 1.3 %fusion.1 = bf16[2,32,4096]{2,1,0:T(8,128)(2,1)S(1)} fusion(s32[1,4,32,4096]{3,2,1,0:T(8,128)} %refs_2_.10, s32[]{:T(128)S(6)} %select_n.30), kind=kLoop, calls=%fused_computation.3 | loop fusion | flops 262144 | bytes 1572868 | tf_op jit(solution)/shard_map/convert_element_type | solution.py:350
  3.4 0.2 collective-permute-start.3
  4.2 0.0 collective-permute-done.2.refs_3_
  4.2 0.0 copy-done.8
  4.2 0.0 copy-done.7
  4.2 0.0 copy-done.6
  4.2 0.0 copy-done
  4.2 2.5 %forward_receptor.2.refs_7_.refs_2_ = bf16[33,64,128]{2,1,0:T(8,128)(2,1)S(1)} custom-call(s32[1]{0:T(128)} %bitcast.refs_0_, s32[1]{0:T(128)S(6)} %copy.12.refs_1_, s32[1,4,32,4096]{3,2,1,0:T(8,128)S(1)} %copy-done, bf16[2,32,4096]{2,1,0:T(8,128)(2,1)S(1)} %collective-permute-done.2.refs_3_, bf16[2,80,64]{2,1,0:T(8,128)(2,1)S(1)} %copy-done.8, ...), custom_call_target="tpu_custom_call" | custom-call | flops 207618048 | bytes 2621440 | tf_op jit(solution)/shard_map/forward_receptor/pallas_call | solution.py:159
  6.8 0.0 copy-start.2
  6.8 3.0 %collective-permute-start.6 = (bf16[33,64,128]{2,1,0:T(8,128)(2,1)S(1)}, bf16[33,64,128]{2,1,0:T(8,128)(2,1)}, u32[]{:S(2)}, u32[]{:S(2)}) collective-permute-start(bf16[33,64,128]{2,1,0:T(8,128)(2,1)S(1)} %forward_receptor.2.refs_7_.refs_2_), channel_id=1, source_target_pairs={{0,4},{4,8},{8,12},{12,0},{1,5},{5,9},{9,13},{13,1},{2,6},{6,10},{... | collective-permute-start | bytes 1622024 | tf_op jit(solution)/shard_map/ppermute | solution.py:22
  9.8 0.0 collective-permute-done.3.refs_3_
  9.8 0.0 copy-done.1
  9.8 3.7 %forward_pose.2.refs_7_.refs_4_ = bf16[33,64,128]{2,1,0:T(8,128)(2,1)S(1)} custom-call(s32[1]{0:T(128)} %bitcast.refs_0_, s32[1]{0:T(128)S(6)} %copy.12.refs_1_, s32[1,4,32,4096]{3,2,1,0:T(8,128)S(1)} %copy-done.1, bf16[2,32,4096]{2,1,0:T(8,128)(2,1)S(1)} %collective-permute-done.3.refs_3_, bf16[2,80,64]{2,1,0:T(8,128)(2,1)S(1)} %copy-done.8, ...), custom_call_target="tpu_custom_call" | custom-call | flops 207618048 | bytes 2621440 | tf_op jit(solution)/shard_map/forward_pose/pallas_call | solution.py:159
  13.4 2.5 %forward_receptor.3.refs_7_.refs_3_ = bf16[33,64,128]{2,1,0:T(8,128)(2,1)S(1)} custom-call(s32[1]{0:T(128)} %bitcast.refs_0_, s32[1]{0:T(128)S(6)} %copy.12.refs_1_, s32[1,4,32,4096]{3,2,1,0:T(8,128)S(1)} %copy-done, bf16[2,32,4096]{2,1,0:T(8,128)(2,1)S(1)} %collective-permute-done.2.refs_3_, bf16[2,80,64]{2,1,0:T(8,128)(2,1)S(1)} %copy-done.8, ...), custom_call_target="tpu_custom_call" | custom-call | flops 207618048 | bytes 2621440 | tf_op jit(solution)/shard_map/forward_receptor/pallas_call | solution.py:159
  16.0 0.0 copy-start.4
  16.0 0.0 copy-start.12
  16.0 1.6 %collective-permute-start.7 = (bf16[33,64,128]{2,1,0:T(8,128)(2,1)S(1)}, bf16[33,64,128]{2,1,0:T(8,128)(2,1)}, u32[]{:S(2)}, u32[]{:S(2)}) collective-permute-start(bf16[33,64,128]{2,1,0:T(8,128)(2,1)S(1)} %forward_receptor.3.refs_7_.refs_3_), channel_id=1, source_target_pairs={{0,4},{4,8},{8,12},{12,0},{1,5},{5,9},{9,13},{13,1},{2,6},{6,10},{... | collective-permute-start | bytes 1622024 | tf_op jit(solution)/shard_map/ppermute | solution.py:22
  17.6 3.7 %forward_pose.3.refs_1_.refs_5_ = bf16[33,64,128]{2,1,0:T(8,128)(2,1)S(1)} custom-call(s32[1]{0:T(128)} %bitcast.refs_0_, s32[1]{0:T(128)S(6)} %copy.12.refs_1_, s32[1,4,32,4096]{3,2,1,0:T(8,128)S(1)} %copy-done.1, bf16[2,32,4096]{2,1,0:T(8,128)(2,1)S(1)} %collective-permute-done.3.refs_3_, bf16[2,80,64]{2,1,0:T(8,128)(2,1)S(1)} %copy-done.8, ...), custom_call_target="tpu_custom_call" | custom-call | flops 207618048 | bytes 2621440 | tf_op jit(solution)/shard_map/forward_pose/pallas_call | solution.py:159
  21.3 0.1 collective-permute-start.5
  21.4 2.0 %collective-permute-start.4 = (bf16[33,64,128]{2,1,0:T(8,128)(2,1)S(1)}, bf16[33,64,128]{2,1,0:T(8,128)(2,1)S(1)}, u32[]{:S(2)}, u32[]{:S(2)}) collective-permute-start(bf16[33,64,128]{2,1,0:T(8,128)(2,1)S(1)} %forward_pose.2.refs_7_.refs_4_), channel_id=1, source_target_pairs={{0,2},{2,0},{1,3},{3,1},{4,6},{6,4},{5,7},{7,5},{8,10},{10,8},{9,1... | collective-permute-start | bytes 1622024 | tf_op jit(solution)/shard_map/ppermute | solution.py:22
  23.4 1.6 %collective-permute-done.6.refs_0_.refs_2_ = bf16[33,64,128]{2,1,0:T(8,128)(2,1)} collective-permute-done((bf16[33,64,128]{2,1,0:T(8,128)(2,1)S(1)}, bf16[33,64,128]{2,1,0:T(8,128)(2,1)}, u32[]{:S(2)}, u32[]{:S(2)}) %collective-permute-start.6) | collective-permute-done | bytes 540704 | tf_op jit(solution)/shard_map/ppermute | solution.py:22
  25.0 11.1 %collective-permute-done.7.refs_0_.refs_3_ = bf16[33,64,128]{2,1,0:T(8,128)(2,1)} collective-permute-done((bf16[33,64,128]{2,1,0:T(8,128)(2,1)S(1)}, bf16[33,64,128]{2,1,0:T(8,128)(2,1)}, u32[]{:S(2)}, u32[]{:S(2)}) %collective-permute-start.7) | collective-permute-done | bytes 540704 | tf_op jit(solution)/shard_map/ppermute | solution.py:22
  36.1 0.4 collective-permute-done.5.refs_7_
  36.5 10.2 %collective-permute-done.4.refs_6_ = bf16[33,64,128]{2,1,0:T(8,128)(2,1)S(1)} collective-permute-done((bf16[33,64,128]{2,1,0:T(8,128)(2,1)S(1)}, bf16[33,64,128]{2,1,0:T(8,128)(2,1)S(1)}, u32[]{:S(2)}, u32[]{:S(2)}) %collective-permute-start.4) | collective-permute-done | bytes 540704 | tf_op jit(solution)/shard_map/ppermute | solution.py:22
  46.7 0.0 copy-done.12
  46.7 3.6 %cross_send.3.refs_8_ = bf16[33,64,128]{2,1,0:T(8,128)(2,1)} custom-call(s32[1]{0:T(128)} %bitcast.refs_0_, f32[4]{0:T(128)S(1)} %copy-done.12, bf16[33,64,128]{2,1,0:T(8,128)(2,1)} %collective-permute-done.6.refs_0_.refs_2_, bf16[33,64,128]{2,1,0:T(8,128)(2,1)} %collective-permute-done.7.refs_0_.refs_3_, ...), custom_call_target="tpu_custom_call" | custom-call | flops 5406720 | bytes 3784704 | tf_op jit(solution)/shard_map/cross_send/pallas_call | solution.py:240
  50.4 0.0 collective-permute-start.9
  50.4 2.9 %cross_keep.3.refs_8_.refs_0_ = f32[33,64,128]{2,1,0:T(8,128)S(1)} custom-call(s32[1]{0:T(128)} %bitcast.refs_0_, f32[4]{0:T(128)S(1)} %copy-done.12, bf16[33,64,128]{2,1,0:T(8,128)(2,1)} %collective-permute-done.6.refs_0_.refs_2_, bf16[33,64,128]{2,1,0:T(8,128)(2,1)} %collective-permute-done.7.refs_0_.refs_3_, ...), custom_call_target="tpu_custom_call" | custom-call | flops 5406720 | bytes 3784704 | tf_op jit(solution)/shard_map/cross_keep/pallas_call | solution.py:240
  53.3 0.0 copy-done.2
  53.3 0.0 copy-done.4
  53.3 2.8 %cross_send.4.refs_8_ = bf16[33,64,128]{2,1,0:T(8,128)(2,1)} custom-call(s32[1]{0:T(128)} %bitcast.refs_0_, f32[4]{0:T(128)S(1)} %copy-done.12, bf16[33,64,128]{2,1,0:T(8,128)(2,1)S(1)} %forward_receptor.2.refs_7_.refs_2_, bf16[33,64,128]{2,1,0:T(8,128)(2,1)S(1)} %forward_receptor.3.refs_7_.refs_3_, bf16[33,64,128]{2,1,0:T(8,128)(2,1)S(1)} %forward_pose.2.refs_7_.refs_4_, ...), custom_call_target="tpu_custom_call" | custom-call | flops 5406720 | bytes 3784704 | tf_op jit(solution)/shard_map/cross_send/pallas_call | solution.py:240
  56.1 0.5 collective-permute-start.8
  56.6 0.5 collective-permute-start.11
  57.0 0.3 collective-permute-start.10
  57.4 2.6 %collective-permute-start = (s32[1]{0:T(128)}, s32[1]{0:T(128)}, u32[]{:S(2)}, u32[]{:S(2)}) collective-permute-start(s32[1]{0:T(128)} %param.14), channel_id=1, source_target_pairs={{0,4},{4,8},{8,12},{12,0},{1,5},{5,9},{9,13},{13,1},{2,6},{6,10},{... | collective-permute-start | bytes 20 | tf_op jit(solution)/shard_map/ppermute | solution.py:22
  60.6 0.0 copy-start.3
  60.7 1.0 %copy-done.3 = bf16[33,64,128]{2,1,0:T(8,128)(2,1)S(1)} copy-done((bf16[33,64,128]{2,1,0:T(8,128)(2,1)S(1)}, bf16[33,64,128]{2,1,0:T(8,128)(2,1)}, u32[]{:S(2)}) %copy-start.3) | copy-done | bytes 540696
  61.7 1.0 %copy-done.5 = bf16[33,64,128]{2,1,0:T(8,128)(2,1)S(1)} copy-done((bf16[33,64,128]{2,1,0:T(8,128)(2,1)S(1)}, bf16[33,64,128]{2,1,0:T(8,128)(2,1)}, u32[]{:S(2)}) %copy-start.5) | copy-done | bytes 540696
  62.8 1.8 %cross_keep.4.refs_5_.refs_0_ = f32[33,64,128]{2,1,0:T(8,128)S(1)} custom-call(s32[1]{0:T(128)} %bitcast.refs_0_, f32[4]{0:T(128)S(1)} %copy-done.12, bf16[33,64,128]{2,1,0:T(8,128)(2,1)S(1)} %copy-done.3, bf16[33,64,128]{2,1,0:T(8,128)(2,1)S(1)} %copy-done.5, bf16[33,64,128]{2,1,0:T(8,128)(2,1)S(1)} %forward_pose.2.refs_7_.refs_4_, ...), custom_call_target="tpu_custom_call" | custom-call | flops 5406720 | bytes 3784704 | tf_op jit(solution)/shard_map/cross_keep/pallas_call | solution.py:240
  64.6 0.0 collective-permute-done.9.refs_1_
  64.6 1.5 %collective-permute-start.1 = (s32[1]{0:T(128)}, s32[1]{0:T(128)}, u32[]{:S(2)}, u32[]{:S(2)}) collective-permute-start(s32[1]{0:T(128)} %param.14), channel_id=1, source_target_pairs={{0,8},{4,12},{8,0},{12,4},{1,9},{5,13},{9,1},{13,5},{2,10},{6,14},... | collective-permute-start | bytes 20 | tf_op jit(solution)/shard_map/ppermute | solution.py:22
  66.2 0.0 copy-done.10
  66.2 3.5 %inverse_pair.3.refs_5_ = f32[1,64]{1,0:T(1,128)S(1)} custom-call(f32[33,64,128]{2,1,0:T(8,128)S(1)} %cross_keep.3.refs_8_.refs_0_, bf16[33,64,128]{2,1,0:T(8,128)(2,1)} %collective-permute-done.9.refs_1_, bf16[64,80]{1,0:T(8,128)(2,1)S(1)} %copy-done.11, bf16[128,64]{1,0:T(8,128)(2,1)S(1)} %copy-done.10, bf16[256,128]{1,0:T(8,128)(2,1)S(1)} %copy-done.9, ...), custom_call_target="tpu_custom_call" | custom-call | flops 207618048 | bytes 4325376 | tf_op jit(solution)/shard_map/inverse_pair/pallas_call | solution.py:300
  69.7 0.0 collective-permute-done.8.refs_1_
  69.7 3.5 %inverse_pair.4.refs_8_ = f32[1,64]{1,0:T(1,128)S(1)} custom-call(f32[33,64,128]{2,1,0:T(8,128)S(1)} %cross_keep.4.refs_5_.refs_0_, bf16[33,64,128]{2,1,0:T(8,128)(2,1)} %collective-permute-done.8.refs_1_, bf16[64,80]{1,0:T(8,128)(2,1)S(1)} %copy-done.11, bf16[128,64]{1,0:T(8,128)(2,1)S(1)} %copy-done.10, bf16[256,128]{1,0:T(8,128)(2,1)S(1)} %copy-done.9, ...), custom_call_target="tpu_custom_call" | custom-call | flops 207618048 | bytes 4325376 | tf_op jit(solution)/shard_map/inverse_pair/pallas_call | solution.py:300
  73.2 0.7 collective-permute-done.11.refs_3_
  73.9 10.6 %collective-permute-done.10.refs_2_ = bf16[33,64,128]{2,1,0:T(8,128)(2,1)} collective-permute-done((bf16[33,64,128]{2,1,0:T(8,128)(2,1)}, bf16[33,64,128]{2,1,0:T(8,128)(2,1)}, u32[]{:S(2)}, u32[]{:S(2)}) %collective-permute-start.10) | collective-permute-done | bytes 540704 | tf_op jit(solution)/shard_map/ppermute | solution.py:22
  84.5 2.9 %cross_send.5.refs_8_ = bf16[33,64,128]{2,1,0:T(8,128)(2,1)S(1)} custom-call(s32[1]{0:T(128)} %bitcast.refs_0_, f32[4]{0:T(128)S(1)} %copy-done.12, bf16[33,64,128]{2,1,0:T(8,128)(2,1)} %collective-permute-done.10.refs_2_, bf16[33,64,128]{2,1,0:T(8,128)(2,1)} %collective-permute-done.11.refs_3_, bf16[33,64,128]{2,1,0:T(8,128)(2,1)S(1)} %forward_pose.2.refs_7_.refs_4_, ...), custom_call_target="tpu_custom_call" | custom-call | flops 5406720 | bytes 3784704 | tf_op jit(solution)/shard_map/cross_send/pallas_call | solution.py:240
  87.4 0.1 collective-permute-start.12
  87.5 0.0 collective-permute-done
  87.5 0.0 collective-permute-done.1
  87.5 1.3 %pad_add_fusion = s32[3]{0:T(128)S(1)} fusion(s32[1]{0:T(128)} %collective-permute-done.1, s32[1]{0:T(128)} %collective-permute-done, s32[1]{0:T(128)S(6)} %copy.13), kind=kLoop, calls=%fused_computation.9 | loop fusion | flops 6 | bytes 24 | tf_op jit(solution)/shard_map/concatenate | solution.py:409
  88.8 0.1 broadcast_compare_fusion
  88.9 2.9 %cross_keep.5.refs_0_.refs_5_ = f32[33,64,128]{2,1,0:T(8,128)S(1)} custom-call(s32[1]{0:T(128)} %bitcast.refs_0_, f32[4]{0:T(128)S(1)} %copy-done.12, bf16[33,64,128]{2,1,0:T(8,128)(2,1)} %collective-permute-done.10.refs_2_, bf16[33,64,128]{2,1,0:T(8,128)(2,1)} %collective-permute-done.11.refs_3_, bf16[33,64,128]{2,1,0:T(8,128)(2,1)S(1)} %forward_pose.2.refs_7_.refs_4_, ...), custom_call_target="tpu_custom_call" | custom-call | flops 5406720 | bytes 3784704 | tf_op jit(solution)/shard_map/cross_keep/pallas_call | solution.py:240
  91.8 0.0 collective-permute-done.12.refs_1_
  91.8 2.5 %inverse_pair.5 = f32[1,64]{1,0:T(1,128)S(1)} custom-call(f32[33,64,128]{2,1,0:T(8,128)S(1)} %cross_keep.5.refs_0_.refs_5_, bf16[33,64,128]{2,1,0:T(8,128)(2,1)S(1)} %collective-permute-done.12.refs_1_, bf16[64,80]{1,0:T(8,128)(2,1)S(1)} %copy-done.11, bf16[128,64]{1,0:T(8,128)(2,1)S(1)} %copy-done.10, bf16[256,128]{1,0:T(8,128)(2,1)S(1)} %copy-done.9, ...), custom_call_target="tpu_custom_call" | custom-call | flops 207618048 | bytes 4325376 | tf_op jit(solution)/shard_map/inverse_pair/pallas_call | solution.py:300
  94.3 0.5 collective-permute-start.13
  94.9 0.1 constant_dynamic-slice_fusion.1
  94.9 0.7 collective-permute-done.13
  95.7 0.1 constant_dynamic-slice_fusion
  95.7 0.7 select_select_fusion
  (15 shorter events, 0.0 us)
Async XLA Ops:
  0.0 4.2 %copy-start.8 = (bf16[2,80,64]{2,1,0:T(8,128)(2,1)S(1)}, bf16[2,80,64]{2,1,0:T(8,128)(2,1)}, u32[]{:S(2)}) copy-start(bf16[2,80,64]{2,1,0:T(8,128)(2,1)} %constant.32.clone.refs_4_) | copy-start | bytes 61444
  0.0 4.2 %copy-start.7 = (bf16[2,128,64]{2,1,0:T(8,128)(2,1)S(1)}, bf16[2,128,64]{2,1,0:T(8,128)(2,1)}, u32[]{:S(2)}) copy-start(bf16[2,128,64]{2,1,0:T(8,128)(2,1)} %constant.33.clone.refs_5_) | copy-start | bytes 98308
  0.0 4.2 %copy-start.6 = (bf16[2,256,128]{2,1,0:T(8,128)(2,1)S(1)}, bf16[2,256,128]{2,1,0:T(8,128)(2,1)}, u32[]{:S(2)}) copy-start(bf16[2,256,128]{2,1,0:T(8,128)(2,1)} %constant.34.clone.refs_6_) | copy-start | bytes 393220
  0.0 4.2 %copy-start = (s32[1,4,32,4096]{3,2,1,0:T(8,128)S(1)}, s32[1,4,32,4096]{3,2,1,0:T(8,128)}, u32[]{:S(2)}) copy-start(s32[1,4,32,4096]{3,2,1,0:T(8,128)} %refs_2_.9) | copy-start | bytes 6291460
  1.4 8.3 %copy-start.1 = (s32[1,4,32,4096]{3,2,1,0:T(8,128)S(1)}, s32[1,4,32,4096]{3,2,1,0:T(8,128)}, u32[]{:S(2)}) copy-start(s32[1,4,32,4096]{3,2,1,0:T(8,128)} %refs_2_.10) | copy-start | bytes 6291460
  1.5 2.7 %collective-permute-start.2 = (bf16[2,32,4096]{2,1,0:T(8,128)(2,1)S(1)}, bf16[2,32,4096]{2,1,0:T(8,128)(2,1)S(1)}, u32[]{:S(2)}, u32[]{:S(2)}) collective-permute-start(bf16[2,32,4096]{2,1,0:T(8,128)(2,1)S(1)} %fusion), channel_id=1, source_target_pairs={{0,1},{1,0},{2,3},{3,2},{4,5},{5,4},{6,7},{7,6},{8,9},{9,8},{10,11... | collective-permute-start | bytes 1572872 | tf_op jit(solution)/shard_map/ppermute | solution.py:22
  3.4 6.4 %collective-permute-start.3 = (bf16[2,32,4096]{2,1,0:T(8,128)(2,1)S(1)}, bf16[2,32,4096]{2,1,0:T(8,128)(2,1)S(1)}, u32[]{:S(2)}, u32[]{:S(2)}) collective-permute-start(bf16[2,32,4096]{2,1,0:T(8,128)(2,1)S(1)} %fusion.1), channel_id=1, source_target_pairs={{0,1},{1,0},{2,3},{3,2},{4,5},{5,4},{6,7},{7,6},{8,9},{9,8},{10,11... | collective-permute-start | bytes 1572872 | tf_op jit(solution)/shard_map/ppermute | solution.py:22
  6.8 46.5 %copy-start.2 = (bf16[33,64,128]{2,1,0:T(8,128)(2,1)}, bf16[33,64,128]{2,1,0:T(8,128)(2,1)S(1)}, u32[]{:S(2)}) copy-start(bf16[33,64,128]{2,1,0:T(8,128)(2,1)S(1)} %forward_receptor.2.refs_7_.refs_2_) | copy-start | bytes 1622020
  6.8 18.2 %collective-permute-start.6 = (bf16[33,64,128]{2,1,0:T(8,128)(2,1)S(1)}, bf16[33,64,128]{2,1,0:T(8,128)(2,1)}, u32[]{:S(2)}, u32[]{:S(2)}) collective-permute-start(bf16[33,64,128]{2,1,0:T(8,128)(2,1)S(1)} %forward_receptor.2.refs_7_.refs_2_), channel_id=1, source_target_pairs={{0,4},{4,8},{8,12},{12,0},{1,5},{5,9},{9,13},{13,1},{2,6},{6,10},{... | collective-permute-start | bytes 1622024 | tf_op jit(solution)/shard_map/ppermute | solution.py:22
  16.0 37.3 %copy-start.4 = (bf16[33,64,128]{2,1,0:T(8,128)(2,1)}, bf16[33,64,128]{2,1,0:T(8,128)(2,1)S(1)}, u32[]{:S(2)}) copy-start(bf16[33,64,128]{2,1,0:T(8,128)(2,1)S(1)} %forward_receptor.3.refs_7_.refs_3_) | copy-start | bytes 1622020
  16.0 30.8 %copy-start.12 = (f32[4]{0:T(128)S(1)}, f32[4]{0:T(128)}, u32[]{:S(2)}) copy-start(f32[4]{0:T(128)} %refs_1_.15) | copy-start | bytes 52
  16.0 20.1 %collective-permute-start.7 = (bf16[33,64,128]{2,1,0:T(8,128)(2,1)S(1)}, bf16[33,64,128]{2,1,0:T(8,128)(2,1)}, u32[]{:S(2)}, u32[]{:S(2)}) collective-permute-start(bf16[33,64,128]{2,1,0:T(8,128)(2,1)S(1)} %forward_receptor.3.refs_7_.refs_3_), channel_id=1, source_target_pairs={{0,4},{4,8},{8,12},{12,0},{1,5},{5,9},{9,13},{13,1},{2,6},{6,10},{... | collective-permute-start | bytes 1622024 | tf_op jit(solution)/shard_map/ppermute | solution.py:22
  21.3 15.2 %collective-permute-start.5 = (bf16[33,64,128]{2,1,0:T(8,128)(2,1)S(1)}, bf16[33,64,128]{2,1,0:T(8,128)(2,1)S(1)}, u32[]{:S(2)}, u32[]{:S(2)}) collective-permute-start(bf16[33,64,128]{2,1,0:T(8,128)(2,1)S(1)} %forward_pose.3.refs_1_.refs_5_), channel_id=1, source_target_pairs={{0,2},{2,0},{1,3},{3,1},{4,6},{6,4},{5,7},{7,5},{8,10},{10,8},{9,1... | collective-permute-start | bytes 1622024 | tf_op jit(solution)/shard_map/ppermute | solution.py:22
  21.4 25.4 %collective-permute-start.4 = (bf16[33,64,128]{2,1,0:T(8,128)(2,1)S(1)}, bf16[33,64,128]{2,1,0:T(8,128)(2,1)S(1)}, u32[]{:S(2)}, u32[]{:S(2)}) collective-permute-start(bf16[33,64,128]{2,1,0:T(8,128)(2,1)S(1)} %forward_pose.2.refs_7_.refs_4_), channel_id=1, source_target_pairs={{0,2},{2,0},{1,3},{3,1},{4,6},{6,4},{5,7},{7,5},{8,10},{10,8},{9,1... | collective-permute-start | bytes 1622024 | tf_op jit(solution)/shard_map/ppermute | solution.py:22
  50.4 14.2 %collective-permute-start.9 = (bf16[33,64,128]{2,1,0:T(8,128)(2,1)}, bf16[33,64,128]{2,1,0:T(8,128)(2,1)}, u32[]{:S(2)}, u32[]{:S(2)}) collective-permute-start(bf16[33,64,128]{2,1,0:T(8,128)(2,1)} %cross_send.3.refs_8_), channel_id=1, source_target_pairs={{0,1},{1,0},{2,3},{3,2},{4,5},{5,4},{6,7},{7,6},{8,9},{9,8},{10,11... | collective-permute-start | bytes 1622024 | tf_op jit(solution)/shard_map/ppermute | solution.py:22
  56.1 13.6 %collective-permute-start.8 = (bf16[33,64,128]{2,1,0:T(8,128)(2,1)}, bf16[33,64,128]{2,1,0:T(8,128)(2,1)}, u32[]{:S(2)}, u32[]{:S(2)}) collective-permute-start(bf16[33,64,128]{2,1,0:T(8,128)(2,1)} %cross_send.4.refs_8_), channel_id=1, source_target_pairs={{0,1},{1,0},{2,3},{3,2},{4,5},{5,4},{6,7},{7,6},{8,9},{9,8},{10,11... | collective-permute-start | bytes 1622024 | tf_op jit(solution)/shard_map/ppermute | solution.py:22
  56.6 17.3 %collective-permute-start.11 = (bf16[33,64,128]{2,1,0:T(8,128)(2,1)}, bf16[33,64,128]{2,1,0:T(8,128)(2,1)}, u32[]{:S(2)}, u32[]{:S(2)}) collective-permute-start(bf16[33,64,128]{2,1,0:T(8,128)(2,1)} %collective-permute-done.7.refs_0_.refs_3_), channel_id=1, source_target_pairs={{0,4},{4,8},{8,12},{12,0},{1,5},{5,9},{9,13},{13,1},{2,6},{6,10},{... | collective-permute-start | bytes 1622024 | tf_op jit(solution)/shard_map/ppermute | solution.py:22
  57.0 27.5 %collective-permute-start.10 = (bf16[33,64,128]{2,1,0:T(8,128)(2,1)}, bf16[33,64,128]{2,1,0:T(8,128)(2,1)}, u32[]{:S(2)}, u32[]{:S(2)}) collective-permute-start(bf16[33,64,128]{2,1,0:T(8,128)(2,1)} %collective-permute-done.6.refs_0_.refs_2_), channel_id=1, source_target_pairs={{0,4},{4,8},{8,12},{12,0},{1,5},{5,9},{9,13},{13,1},{2,6},{6,10},{... | collective-permute-start | bytes 1622024 | tf_op jit(solution)/shard_map/ppermute | solution.py:22
  57.4 30.1 %collective-permute-start = (s32[1]{0:T(128)}, s32[1]{0:T(128)}, u32[]{:S(2)}, u32[]{:S(2)}) collective-permute-start(s32[1]{0:T(128)} %param.14), channel_id=1, source_target_pairs={{0,4},{4,8},{8,12},{12,0},{1,5},{5,9},{9,13},{13,1},{2,6},{6,10},{... | collective-permute-start | bytes 20 | tf_op jit(solution)/shard_map/ppermute | solution.py:22
  60.6 1.0 %copy-start.3 = (bf16[33,64,128]{2,1,0:T(8,128)(2,1)S(1)}, bf16[33,64,128]{2,1,0:T(8,128)(2,1)}, u32[]{:S(2)}) copy-start(bf16[33,64,128]{2,1,0:T(8,128)(2,1)} %copy-done.2) | copy-start | bytes 1622020
  61.7 1.0 %copy-start.5 = (bf16[33,64,128]{2,1,0:T(8,128)(2,1)S(1)}, bf16[33,64,128]{2,1,0:T(8,128)(2,1)}, u32[]{:S(2)}) copy-start(bf16[33,64,128]{2,1,0:T(8,128)(2,1)} %copy-done.4) | copy-start | bytes 1622020
  62.7 3.4 %copy-start.9 = (bf16[256,128]{1,0:T(8,128)(2,1)S(1)}, bf16[256,128]{1,0:T(8,128)(2,1)}, u32[]{:S(2)}) copy-start(bf16[256,128]{1,0:T(8,128)(2,1)} %constant.37.clone.refs_4_) | copy-start | bytes 196612
  62.7 3.4 %copy-start.10 = (bf16[128,64]{1,0:T(8,128)(2,1)S(1)}, bf16[128,64]{1,0:T(8,128)(2,1)}, u32[]{:S(2)}) copy-start(bf16[128,64]{1,0:T(8,128)(2,1)} %constant.36.clone.refs_3_) | copy-start | bytes 49156
  62.8 3.4 %copy-start.11 = (bf16[64,80]{1,0:T(8,128)(2,1)S(1)}, bf16[64,80]{1,0:T(8,128)(2,1)}, u32[]{:S(2)}) copy-start(bf16[64,80]{1,0:T(8,128)(2,1)} %constant.35.clone.refs_2_) | copy-start | bytes 30724
  64.6 22.9 %collective-permute-start.1 = (s32[1]{0:T(128)}, s32[1]{0:T(128)}, u32[]{:S(2)}, u32[]{:S(2)}) collective-permute-start(s32[1]{0:T(128)} %param.14), channel_id=1, source_target_pairs={{0,8},{4,12},{8,0},{12,4},{1,9},{5,13},{9,1},{13,5},{2,10},{6,14},... | collective-permute-start | bytes 20 | tf_op jit(solution)/shard_map/ppermute | solution.py:22
  87.4 4.4 %collective-permute-start.12 = (bf16[33,64,128]{2,1,0:T(8,128)(2,1)S(1)}, bf16[33,64,128]{2,1,0:T(8,128)(2,1)S(1)}, u32[]{:S(2)}, u32[]{:S(2)}) collective-permute-start(bf16[33,64,128]{2,1,0:T(8,128)(2,1)S(1)} %cross_send.5.refs_8_), channel_id=1, source_target_pairs={{0,1},{1,0},{2,3},{3,2},{4,5},{5,4},{6,7},{7,6},{8,9},{9,8},{10,11... | collective-permute-start | bytes 1622024 | tf_op jit(solution)/shard_map/ppermute | solution.py:22
  94.3 1.4 %collective-permute-start.13 = (f32[3,64]{1,0:T(4,128)S(1)}, f32[3,64]{1,0:T(4,128)S(1)}, u32[]{:S(2)}, u32[]{:S(2)}) collective-permute-start(f32[3,64]{1,0:T(4,128)S(1)} %pad_maximum_fusion), channel_id=1, source_target_pairs={{0,1},{1,0},{2,3},{3,2},{4,5},{5,4},{6,7},{7,6},{8,9},{9,8},{10,11... | collective-permute-start | bytes 2312 | tf_op jit(solution)/shard_map/ppermute | solution.py:22
